TPU v7x, 32 devices: a whole 2x2x4 slice. The times are simulated.
32 devices in a mesh: seq: 2 (over core), ctx: 4 (over z), fsdp: 4 (over y, x).
Axes of the slice: x: 2, y: 2, z: 4, core: 2. Of those that a mesh axis runs over, the one named last changes fastest.
Arguments:
- inputs: bfloat16 [8, 1024, 640], P(('seq', 'fsdp'), 'ctx'), may hold values from -6 to 6
- positions: int32 [8, 1024], P(('seq', 'fsdp'), 'ctx'), may hold values from 0 to 1023, as said below
- block_ids: int32 [8, 8], P(('seq', 'fsdp'), 'ctx'), may hold values from 0 to 7, as said below
- w_query: bfloat16 [640, 1024], P('fsdp'), may hold values from -0.25 to 0.25
- w_key: bfloat16 [640, 256], P('fsdp'), may hold values from -0.25 to 0.25
- w_value: bfloat16 [640, 256], P('fsdp'), may hold values from -0.25 to 0.25
- w_out: bfloat16 [1024, 640], P('fsdp'), may hold values from -0.1875 to 0.1875
- w_gate: bfloat16 [640, 2048], P(None, 'fsdp'), may hold values from -0.25 to 0.25
- w_up: bfloat16 [640, 2048], P(None, 'fsdp'), may hold values from -0.25 to 0.25
- w_down: bfloat16 [2048, 640], P('fsdp'), may hold values from -0.125 to 0.125
- gain_in: bfloat16 [640], P('fsdp'), may hold values from 0.25 to 1.75
- gain_query: bfloat16 [256], P('fsdp'), may hold values from 0.25 to 1.75
- gain_key: bfloat16 [256], P('fsdp'), may hold values from 0.25 to 1.75
- gain_attn: bfloat16 [640], P('fsdp'), may hold values from 0.25 to 1.75
- gain_pre: bfloat16 [640], P('fsdp'), may hold values from 0.25 to 1.75
- gain_post: bfloat16 [640], P('fsdp'), may hold values from 0.25 to 1.75
- cotangent: bfloat16 [8, 1024, 640], P(('seq', 'fsdp'), 'ctx'), may hold values from -6 to 6
Outputs:
- result: float32 [8, 1024, 640], P(('seq', 'fsdp'), 'ctx')
- input_grad: float32 [8, 1024, 640], P(('seq', 'fsdp'), 'ctx')
- grad_w_query: float32 [640, 1024], P('fsdp')
- grad_w_key: float32 [640, 256], P('fsdp')
- grad_w_value: float32 [640, 256], P('fsdp')
- grad_w_out: float32 [1024, 640], P('fsdp')
- grad_w_gate: float32 [640, 2048], P(None, 'fsdp')
- grad_w_up: float32 [640, 2048], P(None, 'fsdp')
- grad_w_down: float32 [2048, 640], P('fsdp')
- grad_gain_in: float32 [640], P('fsdp')
- grad_gain_query: float32 [256], P('fsdp')
- grad_gain_key: float32 [256], P('fsdp')
- grad_gain_attn: float32 [640], P('fsdp')
- grad_gain_pre: float32 [640], P('fsdp')
- grad_gain_post: float32 [640], P('fsdp')
Inputs may be any that keep to these rules, and one draw needn't show every extreme that they name: `block_ids`: in every sequence the entries at 2 c and 2 c + 1 are b and 7 - b with b below 4, so a sequence's entries are a permutation of its blocks. `positions`: A token's position counts the tokens before it in its document, documents following one another in the order given by order; every document has at most 1024 tokens and the first of each sequence exactly 1024.
All inputs are finite; a program needn't handle non-finite values.
Results may differ from a plain program's by a relative error of at most 0.022.
Values may be sent and summed in bfloat16 or wider, within the bound.
No kernel may reach another device: no remote copies, remote signals or barrier semaphores. Data moves between devices by JAX's collectives and lax.ppermute only.
A program may use at most 192 MiB of HBM per device.

v0:
```python
import jax
import jax.numpy as jnp
from jax import lax
from jax.experimental import pallas as pl
from jax.experimental.pallas import tpu as pltpu
from jax.sharding import PartitionSpec as P

EPS = 1e-06
THETA = 1000000.0
NEG = -1e30
BF = jnp.bfloat16
F32 = jnp.float32


def matmul(left, right):
    return jnp.dot(left, right, preferred_element_type=F32)


def inner_cols(left, right):
    return lax.dot_general(left, right, (((1,), (1,)), ((), ())), preferred_element_type=F32)


def inner_rows(left, right):
    return lax.dot_general(left, right, (((0,), (0,)), ((), ())), preferred_element_type=F32)


def rotate(value, cosine, sine_table):
    half = value.shape[-1] // 2
    first = value[..., :half]
    second = value[..., half:]
    return jnp.concatenate(
        [first * cosine - second * sine_table, second * cosine + first * sine_table], axis=-1
    )


def tables(positions, head_size):
    half = head_size // 2
    freq = 1.0 / THETA ** (jnp.arange(half, dtype=F32) * 2.0 / head_size)
    angle = positions.astype(F32)[:, None] * freq[None, :]
    return (jnp.cos(angle), jnp.sin(angle))


def swap(value, axis, flip, size):
    return lax.ppermute(value, axis, [(i, i ^ flip) for i in range(size)])


def swap_pair(value):
    return swap(value, "seq", 1, 2)


def swap_split(value, axis, size, flip0, flip1):
    perm = [(i, i ^ flip0) for i in range(size)]
    perm += [(size + i, size + (i ^ flip1)) for i in range(size)]
    return lax.ppermute(value, ("seq", axis), perm)


def gather4(value, core, axis, size, first, second):
    one = swap(value, axis, first, size)
    two = swap(value, axis, second, size)
    both = swap_split(jnp.where(core == 0, one, two), axis, size, second, first)
    return [value, one, two, both]


def scatter4(blocks, core, axis, size, first, second):
    via = swap_split(blocks[3], axis, size, second, first).astype(F32)
    none = jnp.zeros_like(via)
    one = (blocks[1].astype(F32) + jnp.where(core == 0, via, none)).astype(BF)
    two = (blocks[2].astype(F32) + jnp.where(core == 0, none, via)).astype(BF)
    one = swap(one, axis, first, size).astype(F32)
    two = swap(two, axis, second, size).astype(F32)
    return blocks[0].astype(F32) + one + two


def halves(value, pick):
    rows = value.shape[0] // 2
    keep = lax.dynamic_slice_in_dim(value, pick * rows, rows, 0)
    send = lax.dynamic_slice_in_dim(value, (1 - pick) * rows, rows, 0)
    return keep, send


def join(mine, other, pick):
    return jnp.where(
        pick == 0, jnp.concatenate([mine, other], 0), jnp.concatenate([other, mine], 0)
    )


def ctx_sum(value, size, order):
    if size != 4:
        return lax.psum(value.astype(BF), "ctx")
    place = lax.axis_index("ctx")
    high = place // 2
    odd = lax.rem(place, 2)
    mixed = lax.rem(high + odd, 2)
    steps = [(1, mixed), (3, high)] if order == 0 else [(3, high), (1, mixed)]
    for flip, pick in steps:
        keep, send = halves(value, pick)
        value = keep.astype(F32) + swap(send.astype(BF), "ctx", flip, 4).astype(F32)
    value = value.astype(BF)
    for flip, pick in steps[::-1]:
        value = join(value, swap(value, "ctx", flip, 4), pick)
    return value


def attend_forward(queries, key_rows, values, query_order, key_order, score_scale):
    allowed = key_order[None, :] <= query_order[:, None]
    outputs = []
    logsums = []
    for head_index in range(queries.shape[1]):
        scores = inner_cols(queries[:, head_index], key_rows) * score_scale
        scores = jnp.where(allowed, scores, NEG)
        highest = jnp.max(scores, axis=-1, keepdims=True)
        weights = jnp.exp(scores - highest)
        summed = jnp.sum(weights, axis=-1, keepdims=True)
        probs = (weights / summed).astype(BF)
        outputs.append(matmul(probs, values))
        logsums.append(highest + jnp.log(summed))
    return (jnp.stack(outputs, axis=1), jnp.stack(logsums, axis=1))


def attend_backward(
    queries, key_rows, values, query_order, key_order, score_scale, logsums, out_grad
):
    allowed = key_order[None, :] <= query_order[:, None]
    query_grads = []
    key_grad = jnp.zeros(key_rows.shape, F32)
    value_grad = jnp.zeros(values.shape, F32)
    for head_index in range(queries.shape[1]):
        query_head = queries[:, head_index]
        grad_head = out_grad[:, head_index]
        scores = inner_cols(query_head, key_rows) * score_scale
        scores = jnp.where(allowed, scores, NEG)
        probs = jnp.exp(scores - logsums[:, head_index])
        value_grad = value_grad + inner_rows(probs.astype(BF), grad_head)
        prob_grad = inner_cols(grad_head, values)
        weighted = jnp.sum(probs * prob_grad, axis=-1, keepdims=True)
        score_grad = (probs * (prob_grad - weighted)).astype(BF)
        query_grads.append(matmul(score_grad, key_rows) * score_scale)
        key_grad = key_grad + inner_rows(score_grad, query_head) * score_scale
    return (jnp.stack(query_grads, axis=1), key_grad, value_grad)


def kernel_call(body, outs, args, flops, scratch=(), smem=()):
    nbytes = sum(a.size * a.dtype.itemsize for a in args)
    nbytes += sum(o.size * o.dtype.itemsize for o in outs)
    vmem = pl.BlockSpec(memory_space=pltpu.VMEM)
    return pl.pallas_call(
        body,
        out_shape=outs,
        in_specs=[
            pl.BlockSpec(memory_space=pltpu.SMEM) if i in smem else vmem for i in range(len(args))
        ],
        out_specs=[vmem] * len(outs),
        scratch_shapes=list(scratch),
        compiler_params=pltpu.CompilerParams(vmem_limit_bytes=48 * 1024 * 1024),
        cost_estimate=pl.CostEstimate(flops=flops, bytes_accessed=nbytes, transcendentals=0),
    )(*args)


def shape(dims, kind):
    return jax.ShapeDtypeStruct(dims, kind)


def rms_scale(value):
    return lax.rsqrt(jnp.mean(value * value, axis=-1, keepdims=True) + EPS)


def rms_back(value, inverse, gain, grad):
    scaled = value * inverse
    gain_grad = jnp.sum(grad * scaled, axis=0, keepdims=True)
    weighted = grad * gain
    mean = jnp.mean(weighted * scaled, axis=-1, keepdims=True)
    return inverse * (weighted - scaled * mean), gain_grad


def rows_at(start, size, step):
    return pl.ds(pl.multiple_of(start, step), size)


def key_value(inputs, blocks, norm_in, norm_key, cosine, sine, block_ids):
    rows, width = inputs.shape
    size = norm_key.shape[1]
    shard = width // 4

    def body(x, w0, w1, w2, w3, g_in, g_key, cos, sin, ids, hidden, key_pre, packed, full):
        place = lax.axis_index("fsdp")
        for flip, block in enumerate((w0, w1, w2, w3)):
            full[rows_at((place ^ flip) * shard, shard, 16), :] = block[:shard, :]
        value = x[...].astype(F32)
        hid = (value * rms_scale(value) * g_in[...]).astype(BF)
        hidden[...] = hid
        both = matmul(hid, full[...])
        key = both[:, :size]
        key_pre[...] = key
        turned = rotate(key * rms_scale(key) * g_key[...], cos[...], sin[...])
        packed[:rows, :size] = turned.astype(BF)
        packed[:rows, size:] = both[:, size:].astype(BF)
        row = lax.broadcasted_iota(jnp.int32, (16, 2 * size), 0)
        packed[rows:, :] = jnp.where(row == 0, ids[0, 0], ids[0, 1]).astype(F32).astype(BF)

    outs = [
        shape((rows, width), BF),
        shape((rows, size), F32),
        shape((rows + 16, 2 * size), BF),
        shape((width, 2 * size), BF),
    ]
    args = [inputs, *blocks, norm_in, norm_key, cosine, sine, block_ids]
    return kernel_call(body, outs, args, 4 * rows * width * size, smem=(9,))


def query(hidden, mine, other, norm_query, cosine, sine):
    rows, width = hidden.shape
    size = norm_query.shape[1]
    part, cols = mine[0].shape
    heads = cols // size

    def body(hid, *refs):
        blocks, (g_query, cos, sin, query_pre, queries, full) = refs[:8], refs[8:]
        place = lax.axis_index("fsdp")
        core = lax.axis_index("seq")
        for flip in range(4):
            start = (place ^ flip) * 2
            full[rows_at((start + core) * part, part, 16), :] = blocks[flip][...]
            full[rows_at((start + 1 - core) * part, part, 16), :] = blocks[4 + flip][...]
        for head in range(heads):
            at = slice(head * size, (head + 1) * size)
            value = matmul(hid[...], full[:, at])
            query_pre[:, at] = value
            turned = rotate(value * rms_scale(value) * g_query[...], cos[...], sin[...])
            queries[head] = turned.astype(BF)

    outs = [
        shape((rows, cols), F32),
        shape((heads, rows, size), BF),
        shape((width, cols), BF),
    ]
    args = [hidden, *mine, *other, norm_query, cosine, sine]
    return kernel_call(body, outs, args, 2 * rows * width * cols)


def tile_masks(blocks, rows):
    half = rows // 2
    lane = lax.broadcasted_iota(jnp.int32, (1, half), 1).astype(F32)
    row = lax.broadcasted_iota(jnp.int32, (rows, 1), 0)
    own = blocks[0][rows : rows + 16, :half].astype(F32)
    low, high = own[0:1, 0:1], own[1:2, 0:1]
    query_order = jnp.where(row < half, low, high) * half
    query_order = query_order + jnp.where(row < half, row, row - half).astype(F32)
    masks = []
    for block in blocks:
        ids = block[rows : rows + 16, :half].astype(F32)
        keys = jnp.concatenate([ids[0:1] * half + lane, ids[1:2] * half + lane], 1)
        masks.append(keys <= query_order)
    return masks


def attend_kernel(queries, kv_blocks, score_scale):
    heads, rows, size = queries.shape
    count = len(kv_blocks)

    def body(*refs):
        q, blocks, (context, logsum) = refs[0], refs[1 : 1 + count], refs[1 + count :]
        masks = tile_masks(blocks, rows)
        for head in range(heads):
            scores = [
                jnp.where(mask, inner_cols(q[head], block[:rows, :size]) * score_scale, NEG)
                for block, mask in zip(blocks, masks)
            ]
            highest = scores[0].max(-1, keepdims=True)
            for tile in scores[1:]:
                highest = jnp.maximum(highest, tile.max(-1, keepdims=True))
            weights = [jnp.exp(tile - highest) for tile in scores]
            summed = sum(tile.sum(-1, keepdims=True) for tile in weights)
            inverse = 1.0 / summed
            out = sum(
                matmul((tile * inverse).astype(BF), block[:rows, size:])
                for tile, block in zip(weights, blocks)
            )
            context[head] = out.astype(BF)
            logsum[head] = highest + jnp.log(summed)

    outs = [shape((heads, rows, size), BF), shape((heads, rows, 1), F32)]
    return kernel_call(body, outs, [queries, *kv_blocks], 4 * heads * rows * rows * count * size)


def attend_back_kernel(queries, kv_blocks, logsum, out_grad, score_scale):
    heads, rows, size = queries.shape
    count = len(kv_blocks)

    def body(*refs):
        q, blocks, refs = refs[0], refs[1 : 1 + count], refs[1 + count :]
        lse, grads, query_grad, kv_grads, kv_acc = refs[0], refs[1], refs[2], refs[3:-1], refs[-1]
        masks = tile_masks(blocks, rows)
        for head in range(heads):
            q_head, g_head = q[head], grads[head]
            low = lse[head]
            probs = [
                jnp.exp(
                    jnp.where(mask, inner_cols(q_head, block[:rows, :size]) * score_scale, NEG)
                    - low
                )
                for block, mask in zip(blocks, masks)
            ]
            prob_grads = [inner_cols(g_head, block[:rows, size:]) for block in blocks]
            weighted = sum(
                (a * b).sum(-1, keepdims=True) for a, b in zip(probs, prob_grads)
            )
            total = None
            for i, (prob, grad, block) in enumerate(zip(probs, prob_grads, blocks)):
                score_grad = (prob * (grad - weighted)).astype(BF)
                part = matmul(score_grad, block[:rows, :size])
                total = part if total is None else total + part
                key_part = inner_rows(score_grad, q_head) * score_scale
                value_part = inner_rows(prob.astype(BF), g_head)
                if head == 0:
                    kv_acc[i, :, :size] = key_part
                    kv_acc[i, :, size:] = value_part
                else:
                    kv_acc[i, :, :size] += key_part
                    kv_acc[i, :, size:] += value_part
            query_grad[head] = total * score_scale
        for i in range(count):
            kv_grads[i][...] = kv_acc[i].astype(BF)

    outs = [shape((heads, rows, size), F32)] + [shape((rows, 2 * size), BF)] * count
    return kernel_call(
        body,
        outs,
        [queries, *kv_blocks, logsum, out_grad],
        10 * heads * rows * rows * count * size,
        scratch=[pltpu.VMEM((count, rows, 2 * size), F32)],
    )


def gelu_parts(value):
    scale = (2.0 / jnp.pi) ** 0.5
    square = value * value
    tanh = jnp.tanh(scale * (value + 0.044715 * square * value))
    half = 0.5 * (1.0 + tanh)
    slope = half + 0.5 * value * (1.0 - tanh * tanh) * scale * (1.0 + 3 * 0.044715 * square)
    return value * half, slope


def feed_forward(
    inputs, cotangent, context, out_mine, out_other, gate_up, down, norm_attn, norm_pre, norm_post
):
    heads, rows, size = context.shape
    width = inputs.shape[1]
    unit = down[0].shape[0]
    half = size // 2
    count = len(down)
    hidden = unit * count // 2
    offs = [0, width, 2 * width, 3 * width]
    offs += [offs[3] + hidden, offs[3] + 2 * hidden, offs[3] + 3 * hidden]
    total_cols = offs[6] + heads * half

    def body(x, cot, ctx, *refs):
        om, oo, gu, dn = refs[:4], refs[4:8], refs[8 : 8 + count], refs[8 + count : 8 + 2 * count]
        refs = refs[8 + 2 * count :]
        g_attn, g_pre, g_post = refs[0][...], refs[1][...], refs[2][...]
        result, middle_grad, own, send, ctx_grad, gain_grads = refs[3:9]
        w_out, gate, up = refs[9:]
        place = lax.axis_index("fsdp")
        core = lax.axis_index("seq")
        attn_out = None
        for flip in range(4):
            w_out[flip, rows_at(core * half, half, 16), :] = om[flip][...]
            w_out[flip, rows_at((1 - core) * half, half, 16), :] = oo[flip][...]
            value = ctx[place ^ flip]
            low, high = value[:, :half], value[:, half:]
            at = slice(offs[6] + flip * half, offs[6] + (flip + 1) * half)
            own[:, at] = jnp.where(core == 0, low, high)
            send[:, at] = jnp.where(core == 0, high, low)
            part = matmul(value, w_out[flip])
            attn_out = part if attn_out is None else attn_out + part
        inv_attn = rms_scale(attn_out)
        middle = x[...].astype(F32) + attn_out * inv_attn * g_attn
        inv_pre = rms_scale(middle)
        ffn_in = (middle * inv_pre * g_pre).astype(BF)
        own[:, : offs[1]] = ffn_in
        send[:, : offs[1]] = ffn_in
        ffn_out = None
        for i in range(count):
            pre = matmul(ffn_in, gu[i][...])
            gate_pre, up_pre = pre[:, :unit], pre[:, unit:]
            gate[i] = gate_pre
            up[i] = up_pre
            mixed = (gelu_parts(gate_pre)[0] * up_pre).astype(BF)
            j = i % (count // 2)
            dest = own if i < count // 2 else send
            dest[:, offs[3] + j * unit : offs[3] + (j + 1) * unit] = mixed
            part = matmul(mixed, dn[i][...])
            ffn_out = part if ffn_out is None else ffn_out + part
        inv_post = rms_scale(ffn_out)
        result[...] = middle + ffn_out * inv_post * g_post
        grad = cot[...].astype(F32)
        ffn_grad, post_grad = rms_back(ffn_out, inv_post, g_post, grad)
        ffn_grad = ffn_grad.astype(BF)
        own[:, offs[1] : offs[2]] = ffn_grad
        send[:, offs[1] : offs[2]] = ffn_grad
        pre_total = None
        for i in range(count):
            mixed_grad = inner_cols(ffn_grad, dn[i][...])
            activated, slope = gelu_parts(gate[i])
            gate_grad = (mixed_grad * up[i] * slope).astype(BF)
            up_grad = (mixed_grad * activated).astype(BF)
            j = i % (count // 2)
            dest = own if i < count // 2 else send
            dest[:, offs[4] + j * unit : offs[4] + (j + 1) * unit] = gate_grad
            dest[:, offs[5] + j * unit : offs[5] + (j + 1) * unit] = up_grad
            part = inner_cols(gate_grad, gu[i][:, :unit]) + inner_cols(up_grad, gu[i][:, unit:])
            pre_total = part if pre_total is None else pre_total + part
        part, pre_grad = rms_back(middle, inv_pre, g_pre, pre_total)
        mid_grad = grad + part
        middle_grad[...] = mid_grad
        attn_grad, attn_gain = rms_back(attn_out, inv_attn, g_attn, mid_grad)
        attn_grad = attn_grad.astype(BF)
        own[:, offs[2] : offs[3]] = attn_grad
        send[:, offs[2] : offs[3]] = attn_grad
        for flip in range(4):
            ctx_grad[place ^ flip] = inner_cols(attn_grad, w_out[flip]).astype(BF)
        gain_grads[...] = jnp.concatenate(
            [attn_gain, pre_grad, post_grad, jnp.zeros((5, width), F32)], 0
        )

    outs = [
        shape((rows, width), F32),
        shape((rows, width), F32),
        shape((rows, total_cols), BF),
        shape((rows, total_cols), BF),
        shape((heads, rows, size), BF),
        shape((8, width), F32),
    ]
    args = [inputs, cotangent, context, *out_mine, *out_other, *gate_up, *down]
    args += [norm_attn, norm_pre, norm_post]
    scratch = [
        pltpu.VMEM((4, size, width), BF),
        pltpu.VMEM((count, rows, unit), F32),
        pltpu.VMEM((count, rows, unit), F32),
    ]
    flops = 2 * rows * width * (6 * unit * count + 2 * heads * size)
    return kernel_call(body, outs, args, flops, scratch), offs


def ffn_weight_grads(own, got, offs, unit, half):
    rows = own.shape[0]
    width = offs[1]

    def body(a, b, *outs):
        def product(left, right):
            return (
                inner_rows(a[:, left], a[:, right]) + inner_rows(b[:, left], b[:, right])
            ).astype(BF)

        at = lambda k, j, size: slice(offs[k] + j * size, offs[k] + (j + 1) * size)
        whole = lambda k: slice(offs[k], offs[k] + width)
        for j in range(4):
            rest, gate_up = outs[j], outs[4 + j]
            rest[:unit, :] = product(at(3, j, unit), whole(1))
            rest[unit:, :] = product(at(6, j, half), whole(2))
            gate_up[:, :unit] = product(whole(0), at(4, j, unit))
            gate_up[:, unit:] = product(whole(0), at(5, j, unit))

    outs = [shape((unit + half, width), BF)] * 4 + [shape((width, 2 * unit), BF)] * 4
    flops = 4 * rows * width * 4 * (3 * unit + half)
    return kernel_call(body, outs, [own, got], flops)


def query_back(query_grad, query_pre, norm_query, cosine, sine, query_full):
    heads, rows, size = query_grad.shape
    width = query_full.shape[0]
    per = heads // 2

    def body(grad, pre, g_query, cos, sin, full, hidden_part, mine, other, gain_grad):
        core = lax.axis_index("seq")
        gains = None
        outs = []
        total = None
        for head in range(heads):
            at = slice(head * size, (head + 1) * size)
            value = pre[:, at]
            turned = rotate(grad[head], cos[...], -sin[...])
            back, gain = rms_back(value, rms_scale(value), g_query[...], turned)
            gains = gain if gains is None else gains + gain
            outs.append(back.astype(BF))
            part = inner_cols(outs[-1], full[:, at])
            total = part if total is None else total + part
        hidden_part[...] = total
        for head in range(per):
            at = slice(head * size, (head + 1) * size)
            mine[:, at] = jnp.where(core == 0, outs[head], outs[per + head])
            other[:, at] = jnp.where(core == 0, outs[per + head], outs[head])
        gain_grad[...] = gains

    outs = [
        shape((rows, width), F32),
        shape((rows, per * size), BF),
        shape((rows, per * size), BF),
        shape((1, size), F32),
    ]
    args = [query_grad, query_pre, norm_query, cosine, sine, query_full]
    return kernel_call(body, outs, args, 2 * rows * width * heads * size)


def input_back(
    kv_back, key_pre, norm_key, cosine, sine, kv_full, hidden_part, inputs, norm_in, middle_grad,
    hidden, query_mine, query_other,
):
    rows, width = inputs.shape
    size = norm_key.shape[1]
    per = query_mine.shape[1]
    cols = width + per + size

    def body(
        back, k_pre, g_key, cos, sin, full, part, x, g_in, mid, hid, q_mine, q_other,
        input_grad, own, send, in_gain, key_gain,
    ):
        core = lax.axis_index("seq")
        value = k_pre[...]
        turned = rotate(back[:, :size], cos[...], -sin[...])
        key_grad, gain = rms_back(value, rms_scale(value), g_key[...], turned)
        key_gain[...] = gain
        key_grad = key_grad.astype(BF)
        value_grad = back[:, size:].astype(BF)
        total = part[...] + inner_cols(key_grad, full[:, :size])
        total = total + inner_cols(value_grad, full[:, size:])
        value = x[...].astype(F32)
        grad, gain = rms_back(value, rms_scale(value), g_in[...], total)
        input_grad[...] = mid[...] + grad
        in_gain[...] = gain
        own[:, :width] = hid[...]
        send[:, :width] = hid[...]
        own[:, width : width + per] = q_mine[...]
        send[:, width : width + per] = q_other[...]
        own[:, width + per :] = jnp.where(core == 0, key_grad, value_grad)
        send[:, width + per :] = jnp.where(core == 0, value_grad, key_grad)

    outs = [
        shape((rows, width), F32),
        shape((rows, cols), BF),
        shape((rows, cols), BF),
        shape((1, width), F32),
        shape((1, size), F32),
    ]
    args = [kv_back, key_pre, norm_key, cosine, sine, kv_full, hidden_part, inputs, norm_in]
    args += [middle_grad, hidden, query_mine, query_other]
    return kernel_call(body, outs, args, 4 * rows * width * size)


def late_grads(own, got, gains, width):
    rows, cols = own.shape
    out_cols = cols - width
    shard = width // 4

    def body(a, b, extra, *refs):
        outs, total = refs[:4], refs[4]
        place = lax.axis_index("fsdp")
        total[...] = inner_rows(a[:, :width], a[:, width:]) + inner_rows(b[:, :width], b[:, width:])
        for flip, out in enumerate(outs):
            out[:shard, :] = total[rows_at((place ^ flip) * shard, shard, 16), :].astype(BF)
            out[shard:, :] = extra[place ^ flip]

    outs = [shape((shard + gains.shape[1], out_cols), BF)] * 4
    flops = 4 * rows * width * out_cols
    scratch = [pltpu.VMEM((width, out_cols), F32)]
    return kernel_call(body, outs, [own, got, gains], flops, scratch)


def pick_half(value, which, axis):
    size = value.shape[axis] // 2
    return lax.dynamic_slice_in_dim(value, which * size, size, axis)


def join_cols(mine, other, core):
    return jnp.where(
        core == 0, jnp.concatenate([mine, other], 1), jnp.concatenate([other, mine], 1)
    ).astype(F32)


def after(value, *others):
    return lax.optimization_barrier((value,) + others)[0]


def on_device(ctx_size):
    def run(
        inputs,
        positions,
        block_ids,
        w_query,
        w_key,
        w_value,
        w_out,
        w_gate,
        w_up,
        w_down,
        gain_in,
        gain_query,
        gain_key,
        gain_attn,
        gain_pre,
        gain_post,
        cotangent,
    ):
        core = lax.axis_index("seq")
        fsdp = lax.axis_index("fsdp")
        seq_rows, model_width = inputs.shape[1:]
        head_size = gain_query.shape[0] * 4
        half_rows = seq_rows // 2
        score_scale = head_size ** (-0.5)
        inputs, cotangent = inputs[0], cotangent[0]

        gains = [gain_in, gain_attn, gain_pre, gain_post, gain_query, gain_key]
        gain_sizes = [member.shape[0] for member in gains]
        kv_width = 2 * head_size
        shard_rows = w_key.shape[0]
        gain_row = jnp.concatenate(gains)
        gain_row = jnp.pad(gain_row, (0, 16 * kv_width - gain_row.shape[0]))
        packed = jnp.concatenate(
            [jnp.concatenate([w_key, w_value], 1), gain_row.reshape(16, kv_width)], 0
        )
        first = [packed] + [swap(packed, "fsdp", flip, 4) for flip in (1, 2, 3)]
        used = -(-sum(gain_sizes) // kv_width)
        rows = [block[shard_rows : shard_rows + used].astype(F32) for block in first]
        placed = []
        for index in range(4):
            row = rows[0]
            for flip in range(1, 4):
                row = jnp.where((fsdp ^ flip) == index, rows[flip], row)
            placed.append(row.reshape(-1))
        placed = jnp.stack(placed, 0)
        norms = []
        start = 0
        for size in gain_sizes:
            norms.append(placed[:, start : start + size].reshape(1, -1))
            start += size
        norm_in, norm_attn, norm_pre, norm_post, norm_query, norm_key = norms

        def fetch(mine, other):
            mine = gather4(mine, core, "fsdp", 4, 1, 2)
            return mine, [other] + [swap_pair(block) for block in mine[1:]]

        def fetch_half(shard, *order):
            mine, other = pick_half(shard, core, 0), pick_half(shard, 1 - core, 0)
            return fetch(after(mine, *order), other)

        query_mine, query_other = fetch_half(w_query, first[3])
        out_mine, out_other = fetch_half(w_out, query_mine[1], query_mine[2])
        gate_up = jnp.concatenate([pick_half(w_gate, core, 1), pick_half(w_up, core, 1)], 1)
        gate_up_other = jnp.concatenate(
            [pick_half(w_gate, 1 - core, 1), pick_half(w_up, 1 - core, 1)], 1
        )
        gu_mine, gu_other = fetch(after(gate_up, out_mine[1], out_mine[2]), gate_up_other)
        down_mine, down_other = fetch_half(w_down, gu_mine[1], gu_mine[2])
        unit = gate_up.shape[1] // 2

        cosine, sine = tables(positions[0], head_size)
        hidden, key_pre, packed_kv, kv_full = key_value(
            inputs, first, norm_in, norm_key, cosine, sine, block_ids
        )
        if ctx_size == 4:
            kv_blocks = gather4(packed_kv, core, "ctx", 4, 1, 3)
        else:
            kv_all = lax.all_gather(packed_kv, "ctx", axis=0)
        query_pre, queries, query_full = query(
            hidden, query_mine, query_other, norm_query, cosine, sine
        )
        if ctx_size == 4:
            context, logsum = attend_kernel(queries, kv_blocks, score_scale)
        else:
            offsets = jnp.arange(half_rows, dtype=jnp.int32)
            block_all = kv_all[:, seq_rows : seq_rows + 2, 0].astype(jnp.int32)
            key_order = (block_all[:, :, None] * half_rows + offsets).reshape(-1)
            query_order = (block_ids[0][:, None] * half_rows + offsets).reshape(-1)
            key_all = kv_all[:, :seq_rows, :head_size].reshape(-1, head_size)
            value_all = kv_all[:, :seq_rows, head_size:].reshape(-1, head_size)
            by_row = queries.transpose(1, 0, 2)
            seq_out, logsum = attend_forward(
                by_row, key_all, value_all, query_order, key_order, score_scale
            )
            context = seq_out.astype(BF).transpose(1, 0, 2)

        (result, middle_grad, own, send, context_grad, gain_grads), offs = feed_forward(
            inputs,
            cotangent,
            context,
            out_mine,
            out_other,
            gu_mine + gu_other,
            down_mine + down_other,
            norm_attn,
            norm_pre,
            norm_post,
        )

        parts = ffn_weight_grads(own, swap_pair(send), offs, unit, head_size // 2)
        rest_sum = ctx_sum(scatter4(parts[:4], core, "fsdp", 4, 1, 2), ctx_size, 1)
        gu_sum = ctx_sum(scatter4(parts[4:], core, "fsdp", 4, 1, 2), ctx_size, 0)
        rest_other = swap_pair(rest_sum)
        gu_other = swap_pair(gu_sum)
        total_down = join(rest_sum[:unit], rest_other[:unit], core).astype(F32)
        total_out = join(rest_sum[unit:], rest_other[unit:], core).astype(F32)
        total_gate = join_cols(gu_sum[:, :unit], gu_other[:, :unit], core)
        total_up = join_cols(gu_sum[:, unit:], gu_other[:, unit:], core)

        context_grad = after(context_grad, *parts)
        if ctx_size == 4:
            query_grad, *kv_parts = attend_back_kernel(
                queries, kv_blocks, logsum, context_grad, score_scale
            )
            kv_back = scatter4(kv_parts, core, "ctx", 4, 1, 3)
        else:
            query_grad, key_grad, value_grad = attend_backward(
                by_row,
                key_all,
                value_all,
                query_order,
                key_order,
                score_scale,
                logsum,
                context_grad.transpose(1, 0, 2),
            )
            query_grad = query_grad.transpose(1, 0, 2)
            kv_grad = jnp.concatenate([key_grad, value_grad], 1).astype(BF)
            kv_back = lax.psum_scatter(kv_grad, "ctx", scatter_dimension=0, tiled=True).astype(F32)
        hidden_part, back_mine, back_other, grad_query = query_back(
            query_grad, query_pre, norm_query, cosine, sine, query_full
        )
        input_grad, own, send, grad_in, grad_key = input_back(
            kv_back,
            key_pre,
            norm_key,
            cosine,
            sine,
            kv_full,
            hidden_part,
            inputs,
            norm_in,
            middle_grad,
            hidden,
            back_mine,
            back_other,
        )
        gain_list = (grad_in, gain_grads[0], gain_grads[1], gain_grads[2], grad_query, grad_key)
        gain_rows = jnp.concatenate([member.reshape(4, 1, -1) for member in gain_list], 2)
        width = own.shape[1] - model_width
        gain_count = -(-gain_rows.shape[2] // width)
        gain_rows = jnp.pad(gain_rows, ((0, 0), (0, 0), (0, gain_count * width - gain_rows.shape[2])))
        gain_rows = gain_rows.reshape(4, gain_count, width).astype(BF)
        gain_rows = jnp.pad(gain_rows, ((0, 0), (0, 32 - gain_count), (0, 0)))
        late_parts = late_grads(own, swap_pair(send), gain_rows, model_width)
        late_sum = ctx_sum(scatter4(late_parts, core, "fsdp", 4, 1, 2), ctx_size, 0)
        late_other = swap_pair(late_sum)
        query_cols = width - head_size
        total_query = join_cols(
            late_sum[:shard_rows, :query_cols], late_other[:shard_rows, :query_cols], core
        )
        total_key = jnp.where(core == 0, late_sum, late_other)[:shard_rows, query_cols:].astype(F32)
        total_value = jnp.where(core == 0, late_other, late_sum)[:shard_rows, query_cols:].astype(F32)
        gain_at = slice(shard_rows, shard_rows + gain_count)
        gain_total = (late_sum[gain_at].astype(F32) + late_other[gain_at].astype(F32)).reshape(-1)
        outs = []
        start = 0
        for size in gain_sizes:
            outs.append(gain_total[start : start + size])
            start += size
        g_in, g_attn, g_pre, g_post, g_query, g_key = outs
        return (
            result[None],
            input_grad[None],
            total_query,
            total_key,
            total_value,
            total_out,
            total_gate,
            total_up,
            total_down,
            g_in,
            g_query,
            g_key,
            g_attn,
            g_pre,
            g_post,
        )

    return run


def solution(mesh):
    rows = P(("seq", "fsdp"), "ctx")
    wide = P(("seq", "fsdp"), "ctx", None)
    first = P("fsdp", None)
    second = P(None, "fsdp")
    flat = P("fsdp")
    in_specs = (wide, rows, rows, first, first, first, first, second, second, first)
    in_specs += (flat,) * 6 + (wide,)
    out_specs = (wide, wide, first, first, first, first, second, second, first) + (flat,) * 6
    return jax.shard_map(
        on_device(mesh.shape["ctx"]),
        mesh=mesh,
        in_specs=in_specs,
        out_specs=out_specs,
        check_vma=False,
    )
```

profile of v0, /device:TPU:0, one launch (start us, length us, event | category | flops | bytes accessed | tf_op | source)
XLA Modules:
  0.0 241.4 jit_solution(4966571345142970125)
XLA Ops:
  0.7 4.2 %concatenate.106 = bf16[768]{0:T(1024)(128)(2,1)S(1)} concatenate(bf16[160]{0:T(256)(128)(2,1)} %param.27, bf16[160]{0:T(256)(128)(2,1)} %param.30, bf16[160]{0:T(256)(128)(2,1)} %param.31, bf16[160]{0:T(256)(128)(2,1)} %param.32, bf16[64]{0:T(256)(128)(2,1)} %param.28, bf16[64]{0:T(256)(128)(2,1)} %param.29), dimensions={0} | concatenate | bytes 3072 | tf_op jit(solution)/shard_map/concatenate | solution.py:615
  5.8 4.0 %collective-permute-start.2 = (bf16[176,512]{1,0:T(8,128)(2,1)S(1)}, bf16[176,512]{1,0:T(8,128)(2,1)S(1)}, u32[]{:S(2)}, u32[]{:S(2)}) collective-permute-start(bf16[176,512]{1,0:T(8,128)(2,1)S(1)} %pad_maximum_fusion.2.w0), channel_id=1, source_target_pairs={{0,3},{1,2},{2,1},{3,0},{4,7},{5,6},{6,5},{7,4},{8,11},{9,10},{10,... | collective-permute-start | bytes 540680 | tf_op jit(solution)/shard_map/ppermute | solution.py:44
  25.7 3.4 %collective-permute-done.12.refs_1_ = bf16[128,640]{1,0:T(8,128)(2,1)S(1)} collective-permute-done((bf16[128,640]{1,0:T(8,128)(2,1)S(1)}, bf16[128,640]{1,0:T(8,128)(2,1)S(1)}, u32[]{:S(2)}, u32[]{:S(2)}) %collective-permute-start.12) | collective-permute-done | bytes 163872 | tf_op jit(solution)/shard_map/ppermute | solution.py:44
  34.5 3.7 %collective-permute-start.10 = (bf16[272,512]{1,0:T(8,128)(2,1)S(1)}, bf16[272,512]{1,0:T(8,128)(2,1)S(1)}, u32[]{:S(2)}, u32[]{:S(2)}) collective-permute-start(bf16[272,512]{1,0:T(8,128)(2,1)S(1)} %get-tuple-element.64.refs_1_), channel_id=1, source_target_pairs={{0,12},{4,8},{8,4},{12,0},{1,13},{5,9},{9,5},{13,1},{2,14},{6,10},... | collective-permute-start | bytes 835592 | tf_op jit(solution)/shard_map/ppermute | solution.py:44
  38.8 6.1 %collective-permute-done.18.refs_9_ = bf16[640,512]{1,0:T(8,128)(2,1)} collective-permute-done((bf16[640,512]{1,0:T(8,128)(2,1)}, bf16[640,512]{1,0:T(8,128)(2,1)}, u32[]{:S(2)}, u32[]{:S(2)}) %collective-permute-start.18) | collective-permute-done | bytes 655392 | tf_op jit(solution)/shard_map/ppermute | solution.py:44
  53.1 3.6 %collective-permute-start.11 = (bf16[272,512]{1,0:T(8,128)(2,1)S(1)}, bf16[272,512]{1,0:T(8,128)(2,1)S(1)}, u32[]{:S(2)}, u32[]{:S(2)}) collective-permute-start(bf16[272,512]{1,0:T(8,128)(2,1)S(1)} %broadcast_select_fusion.2), channel_id=1, source_target_pairs={{0,12},{4,8},{8,4},{12,0},{16,20},{20,16},{24,28},{28,24},{1,13},{... | collective-permute-start | bytes 835592 | tf_op jit(solution)/shard_map/ppermute | solution.py:54
  56.7 9.8 %collective-permute-done.14.refs_3_ = bf16[128,640]{1,0:T(8,128)(2,1)S(1)} collective-permute-done((bf16[128,640]{1,0:T(8,128)(2,1)S(1)}, bf16[128,640]{1,0:T(8,128)(2,1)S(1)}, u32[]{:S(2)}, u32[]{:S(2)}) %collective-permute-start.14) | collective-permute-done | bytes 163872 | tf_op jit(solution)/shard_map/ppermute | solution.py:54
  73.0 4.1 %collective-permute-done.26.refs_19_ = bf16[256,640]{1,0:T(8,128)(2,1)} collective-permute-done((bf16[256,640]{1,0:T(8,128)(2,1)S(1)}, bf16[256,640]{1,0:T(8,128)(2,1)}, u32[]{:S(2)}, u32[]{:S(2)}) %collective-permute-start.26) | collective-permute-done | bytes 327712 | tf_op jit(solution)/shard_map/ppermute | solution.py:54
  88.4 2.4 shard_map.282
  90.9 15.0 %shard_map.283 = (f32[256,640]{1,0:T(8,128)}, f32[256,640]{1,0:T(8,128)}, bf16[256,5504]{1,0:T(8,128)(2,1)}, bf16[256,5504]{1,0:T(8,128)(2,1)}, bf16[4,256,256]{2,1,0:T(8,128)(2,1)S(1)}, /*index=5*/f32[8,640]{1,0:T(8,128)S(1)}) custom-call(bf16[256,640]{1,0:T(8,128)(2,1)S(1)} %bitcast.30, bf16[256,640]{1,0:T(8,128)(2,1)S(1)} %bitcast.32, ...), custom_call_target="tpu_custom_call" | custom-call | flops 4697620480 | bytes 17853952 | tf_op jit(solution)/shard_map/pallas_call | solution.py:146
  106.0 5.3 %collective-permute-done.30.b = bf16[256,5504]{1,0:T(8,128)(2,1)S(1)} collective-permute-done((bf16[256,5504]{1,0:T(8,128)(2,1)}, bf16[256,5504]{1,0:T(8,128)(2,1)S(1)}, u32[]{:S(2)}, u32[]{:S(2)}) %collective-permute-start.30) | collective-permute-done | bytes 2818080 | tf_op jit(solution)/shard_map/ppermute | solution.py:44
  112.9 6.0 %shard_map.284 = (bf16[384,640]{1,0:T(8,128)(2,1)S(1)}, bf16[384,640]{1,0:T(8,128)(2,1)S(1)}, bf16[384,640]{1,0:T(8,128)(2,1)S(1)}, bf16[384,640]{1,0:T(8,128)(2...) custom-call(bf16[256,5504]{1,0:T(8,128)(2,1)} %get-tuple-element.72., ...), custom_call_target="tpu_custom_call" | custom-call | flops 2348810240 | bytes 10223616 | tf_op jit(solution)/shard_map/pallas_call | solution.py:146
  124.6 5.3 %shard_map.285 = (f32[4,256,256]{2,1,0:T(8,128)S(1)}, bf16[256,512]{1,0:T(8,128)(2,1)S(1)}, bf16[256,512]{1,0:T(8,128)(2,1)S(1)}, bf16[256,512]{1,0:T(8,128)(2,1)S(1)}, bf16[256,512]{1,0:T(8,128)(2,1)}) custom-call(bf16[4,256,256]{2,1,0:T(8,128)(2,1)S(1)} %get-tuple-element.63.refs_0_, bf16[272,512]{1,0:T(8,128)(2,1)S(1)} %copy-done.66, ...), custom_call_target="tpu_custom_call" | custom-call | flops 2684354560 | bytes 4263936 | tf_op jit(solution)/shard_map/pallas_call | solution.py:146
  132.3 3.3 %collective-permute-start.31 = (bf16[256,512]{1,0:T(8,128)(2,1)}, bf16[256,512]{1,0:T(8,128)(2,1)}, u32[]{:S(2)}, u32[]{:S(2)}) collective-permute-start(bf16[256,512]{1,0:T(8,128)(2,1)} %get-tuple-element.85), channel_id=1, source_target_pairs={{0,12},{4,8},{8,4},{12,0},{16,20},{20,16},{24,28},{28,24},{1,13},{... | collective-permute-start | bytes 786440 | tf_op jit(solution)/shard_map/ppermute | solution.py:54
  152.9 6.6 %collective-permute-done.33 = bf16[256,512]{1,0:T(8,128)(2,1)S(1)} collective-permute-done((bf16[256,512]{1,0:T(8,128)(2,1)S(1)}, bf16[256,512]{1,0:T(8,128)(2,1)S(1)}, u32[]{:S(2)}, u32[]{:S(2)}) %collective-permute-start.33) | collective-permute-done | bytes 262176 | tf_op jit(solution)/shard_map/ppermute | solution.py:44
  166.8 8.5 %collective-permute-done.46 = bf16[192,640]{1,0:T(8,128)(2,1)S(1)} collective-permute-done((bf16[192,640]{1,0:T(8,128)(2,1)S(1)}, bf16[192,640]{1,0:T(8,128)(2,1)S(1)}, u32[]{:S(2)}, u32[]{:S(2)}) %collective-permute-start.46) | collective-permute-done | bytes 245792 | tf_op jit(solution)/shard_map/ppermute | solution.py:44
  175.5 4.2 %collective-permute-start.47 = (bf16[96,640]{1,0:T(8,128)(2,1)S(1)}, bf16[96,640]{1,0:T(8,128)(2,1)S(1)}, u32[]{:S(2)}, u32[]{:S(2)}) collective-permute-start(bf16[96,640]{1,0:T(8,128)(2,1)S(1)} %dynamic-slice_convert_fusion.4), channel_id=1, source_target_pairs={{0,4},{4,0},{8,12},{12,8},{1,5},{5,1},{9,13},{13,9},{2,6},{6,2},{1... | collective-permute-start | bytes 368648 | tf_op jit(solution)/shard_map/ppermute | solution.py:44
  184.9 2.4 %collective-permute-done.35 = bf16[192,768]{1,0:T(8,128)(2,1)S(1)} collective-permute-done((bf16[192,768]{1,0:T(8,128)(2,1)S(1)}, bf16[192,768]{1,0:T(8,128)(2,1)S(1)}, u32[]{:S(2)}, u32[]{:S(2)}) %collective-permute-start.35) | collective-permute-done | bytes 294944 | tf_op jit(solution)/shard_map/ppermute | solution.py:54
  189.4 5.0 %collective-permute-done.48 = bf16[96,640]{1,0:T(8,128)(2,1)S(1)} collective-permute-done((bf16[96,640]{1,0:T(8,128)(2,1)S(1)}, bf16[96,640]{1,0:T(8,128)(2,1)S(1)}, u32[]{:S(2)}, u32[]{:S(2)}) %collective-permute-start.48) | collective-permute-done | bytes 122912 | tf_op jit(solution)/shard_map/ppermute | solution.py:44
  196.2 2.6 %collective-permute-start.55 = (bf16[160,512]{1,0:T(8,128)(2,1)S(1)}, bf16[160,512]{1,0:T(8,128)(2,1)S(1)}, u32[]{:S(2)}, u32[]{:S(2)}) collective-permute-start(bf16[160,512]{1,0:T(8,128)(2,1)S(1)} %dynamic-slice_convert_fusion.2), channel_id=1, source_target_pairs={{0,12},{4,8},{8,4},{12,0},{1,13},{5,9},{9,5},{13,1},{2,14},{6,10},... | collective-permute-start | bytes 491528 | tf_op jit(solution)/shard_map/ppermute | solution.py:44
  198.8 6.5 %collective-permute-done.49 = bf16[192,640]{1,0:T(8,128)(2,1)S(1)} collective-permute-done((bf16[192,640]{1,0:T(8,128)(2,1)S(1)}, bf16[192,640]{1,0:T(8,128)(2,1)S(1)}, u32[]{:S(2)}, u32[]{:S(2)}) %collective-permute-start.49) | collective-permute-done | bytes 245792 | tf_op jit(solution)/shard_map/ppermute | solution.py:44
  211.2 2.7 %collective-permute-done.39 = bf16[48,768]{1,0:T(8,128)(2,1)S(1)} collective-permute-done((bf16[48,768]{1,0:T(8,128)(2,1)S(1)}, bf16[48,768]{1,0:T(8,128)(2,1)S(1)}, u32[]{:S(2)}, u32[]{:S(2)}) %collective-permute-start.39) | collective-permute-done | bytes 73760 | tf_op jit(solution)/shard_map/ppermute | solution.py:44
  217.9 9.4 %collective-permute-start.57 = (bf16[320,512]{1,0:T(8,128)(2,1)S(1)}, bf16[320,512]{1,0:T(8,128)(2,1)S(1)}, u32[]{:S(2)}, u32[]{:S(2)}) collective-permute-start(bf16[320,512]{1,0:T(8,128)(2,1)S(1)} %maximum_select_fusion.7), channel_id=1, source_target_pairs={{0,4},{4,0},{8,12},{12,8},{1,5},{5,1},{9,13},{13,9},{2,6},{6,2},{1... | collective-permute-start | bytes 983048 | tf_op jit(solution)/shard_map/ppermute | solution.py:44
  230.2 4.6 %collective-permute-done.41 = bf16[96,768]{1,0:T(8,128)(2,1)S(1)} collective-permute-done((bf16[96,768]{1,0:T(8,128)(2,1)S(1)}, bf16[96,768]{1,0:T(8,128)(2,1)S(1)}, u32[]{:S(2)}, u32[]{:S(2)}) %collective-permute-start.41) | collective-permute-done | bytes 147488 | tf_op jit(solution)/shard_map/ppermute | solution.py:44
  (370 shorter events, 111.2 us)
Async XLA Ops:
  29.1 15.8 %collective-permute-start.18 = (bf16[640,512]{1,0:T(8,128)(2,1)}, bf16[640,512]{1,0:T(8,128)(2,1)}, u32[]{:S(2)}, u32[]{:S(2)}) collective-permute-start(bf16[640,512]{1,0:T(8,128)(2,1)} %pad_maximum_fusion.refs_8_), channel_id=1, source_target_pairs={{0,1},{1,0},{2,3},{3,2},{4,5},{5,4},{6,7},{7,6},{8,9},{9,8},{10,11... | collective-permute-start | bytes 1966088 | tf_op jit(solution)/shard_map/ppermute | solution.py:44
  31.4 13.5 %collective-permute-start.19 = (bf16[640,512]{1,0:T(8,128)(2,1)}, bf16[640,512]{1,0:T(8,128)(2,1)}, u32[]{:S(2)}, u32[]{:S(2)}) collective-permute-start(bf16[640,512]{1,0:T(8,128)(2,1)} %pad_maximum_fusion.refs_8_), channel_id=1, source_target_pairs={{0,2},{1,3},{2,0},{3,1},{4,6},{5,7},{6,4},{7,5},{8,10},{9,11},{10,... | collective-permute-start | bytes 1966088 | tf_op jit(solution)/shard_map/ppermute | solution.py:44
  46.6 19.9 %collective-permute-start.24 = (bf16[256,640]{1,0:T(8,128)(2,1)S(1)}, bf16[256,640]{1,0:T(8,128)(2,1)S(1)}, u32[]{:S(2)}, u32[]{:S(2)}) collective-permute-start(bf16[256,640]{1,0:T(8,128)(2,1)S(1)} %get-tuple-element.68.refs_16_), channel_id=1, source_target_pairs={{0,1},{1,0},{2,3},{3,2},{4,5},{5,4},{6,7},{7,6},{8,9},{9,8},{10,11... | collective-permute-start | bytes 983048 | tf_op jit(solution)/shard_map/ppermute | solution.py:44
  48.2 18.8 %collective-permute-start.25 = (bf16[256,640]{1,0:T(8,128)(2,1)S(1)}, bf16[256,640]{1,0:T(8,128)(2,1)}, u32[]{:S(2)}, u32[]{:S(2)}) collective-permute-start(bf16[256,640]{1,0:T(8,128)(2,1)S(1)} %get-tuple-element.68.refs_16_), channel_id=1, source_target_pairs={{0,2},{1,3},{2,0},{3,1},{4,6},{5,7},{6,4},{7,5},{8,10},{9,11},{10,... | collective-permute-start | bytes 983048 | tf_op jit(solution)/shard_map/ppermute | solution.py:44
  49.5 23.5 %collective-permute-start.20 = (bf16[640,512]{1,0:T(8,128)(2,1)S(1)}, bf16[640,512]{1,0:T(8,128)(2,1)}, u32[]{:S(2)}, u32[]{:S(2)}) collective-permute-start(bf16[640,512]{1,0:T(8,128)(2,1)S(1)} %broadcast_select_fusion), channel_id=1, source_target_pairs={{0,2},{1,3},{2,0},{3,1},{16,17},{17,16},{18,19},{19,18},{4,6},{5,7... | collective-permute-start | bytes 1966088 | tf_op jit(solution)/shard_map/ppermute | solution.py:54
  50.4 16.1 %collective-permute-start.14 = (bf16[128,640]{1,0:T(8,128)(2,1)S(1)}, bf16[128,640]{1,0:T(8,128)(2,1)S(1)}, u32[]{:S(2)}, u32[]{:S(2)}) collective-permute-start(bf16[128,640]{1,0:T(8,128)(2,1)S(1)} %broadcast_select_fusion.3), channel_id=1, source_target_pairs={{0,2},{1,3},{2,0},{3,1},{16,17},{17,16},{18,19},{19,18},{4,6},{5,7... | collective-permute-start | bytes 491528 | tf_op jit(solution)/shard_map/ppermute | solution.py:54
  53.1 18.0 %collective-permute-start.11 = (bf16[272,512]{1,0:T(8,128)(2,1)S(1)}, bf16[272,512]{1,0:T(8,128)(2,1)S(1)}, u32[]{:S(2)}, u32[]{:S(2)}) collective-permute-start(bf16[272,512]{1,0:T(8,128)(2,1)S(1)} %broadcast_select_fusion.2), channel_id=1, source_target_pairs={{0,12},{4,8},{8,4},{12,0},{16,20},{20,16},{24,28},{28,24},{1,13},{... | collective-permute-start | bytes 835592 | tf_op jit(solution)/shard_map/ppermute | solution.py:54
  68.5 22.2 %collective-permute-start.21 = (bf16[640,512]{1,0:T(8,128)(2,1)}, bf16[640,512]{1,0:T(8,128)(2,1)}, u32[]{:S(2)}, u32[]{:S(2)}) collective-permute-start(bf16[640,512]{1,0:T(8,128)(2,1)} %collective-permute-done.18.refs_9_), channel_id=1, source_target_pairs={{0,16},{16,0},{1,17},{17,1},{2,18},{18,2},{3,19},{19,3},{4,20},{20... | collective-permute-start | bytes 1966088 | tf_op jit(solution)/shard_map/ppermute | solution.py:44
  71.8 18.9 %collective-permute-start.22 = (bf16[640,512]{1,0:T(8,128)(2,1)}, bf16[640,512]{1,0:T(8,128)(2,1)}, u32[]{:S(2)}, u32[]{:S(2)}) collective-permute-start(bf16[640,512]{1,0:T(8,128)(2,1)} %collective-permute-done.19.refs_10_), channel_id=1, source_target_pairs={{0,16},{16,0},{1,17},{17,1},{2,18},{18,2},{3,19},{19,3},{4,20},{20... | collective-permute-start | bytes 1966088 | tf_op jit(solution)/shard_map/ppermute | solution.py:44
  73.0 17.8 %collective-permute-start.23 = (bf16[640,512]{1,0:T(8,128)(2,1)}, bf16[640,512]{1,0:T(8,128)(2,1)}, u32[]{:S(2)}, u32[]{:S(2)}) collective-permute-start(bf16[640,512]{1,0:T(8,128)(2,1)} %collective-permute-done.20.refs_11_), channel_id=1, source_target_pairs={{0,16},{16,0},{1,17},{17,1},{2,18},{18,2},{3,19},{19,3},{4,20},{20... | collective-permute-start | bytes 1966088 | tf_op jit(solution)/shard_map/ppermute | solution.py:44
  77.1 13.7 %collective-permute-start.28 = (bf16[256,640]{1,0:T(8,128)(2,1)}, bf16[256,640]{1,0:T(8,128)(2,1)}, u32[]{:S(2)}, u32[]{:S(2)}) collective-permute-start(bf16[256,640]{1,0:T(8,128)(2,1)} %collective-permute-done.25.refs_18_), channel_id=1, source_target_pairs={{0,16},{16,0},{1,17},{17,1},{2,18},{18,2},{3,19},{19,3},{4,20},{20... | collective-permute-start | bytes 983048 | tf_op jit(solution)/shard_map/ppermute | solution.py:44
  77.1 13.7 %collective-permute-start.29 = (bf16[256,640]{1,0:T(8,128)(2,1)}, bf16[256,640]{1,0:T(8,128)(2,1)}, u32[]{:S(2)}, u32[]{:S(2)}) collective-permute-start(bf16[256,640]{1,0:T(8,128)(2,1)} %collective-permute-done.26.refs_19_), channel_id=1, source_target_pairs={{0,16},{16,0},{1,17},{17,1},{2,18},{18,2},{3,19},{19,3},{4,20},{20... | collective-permute-start | bytes 983048 | tf_op jit(solution)/shard_map/ppermute | solution.py:44
  141.9 19.7 %collective-permute-start.51 = (bf16[640,512]{1,0:T(8,128)(2,1)}, bf16[640,512]{1,0:T(8,128)(2,1)S(1)}, u32[]{:S(2)}, u32[]{:S(2)}) collective-permute-start(bf16[640,512]{1,0:T(8,128)(2,1)} %copy-done.60), channel_id=1, source_target_pairs={{0,2},{1,3},{2,0},{3,1},{16,17},{17,16},{18,19},{19,18},{4,6},{5,7... | collective-permute-start | bytes 1966088 | tf_op jit(solution)/shard_map/ppermute | solution.py:54
  146.4 13.2 %collective-permute-start.33 = (bf16[256,512]{1,0:T(8,128)(2,1)S(1)}, bf16[256,512]{1,0:T(8,128)(2,1)S(1)}, u32[]{:S(2)}, u32[]{:S(2)}) collective-permute-start(bf16[256,512]{1,0:T(8,128)(2,1)S(1)} %get-tuple-element.136), channel_id=1, source_target_pairs={{0,12},{4,8},{8,4},{12,0},{1,13},{5,9},{9,5},{13,1},{2,14},{6,10},... | collective-permute-start | bytes 786440 | tf_op jit(solution)/shard_map/ppermute | solution.py:44
  148.5 16.8 %collective-permute-start.44 = (bf16[384,640]{1,0:T(8,128)(2,1)S(1)}, bf16[384,640]{1,0:T(8,128)(2,1)S(1)}, u32[]{:S(2)}, u32[]{:S(2)}) collective-permute-start(bf16[384,640]{1,0:T(8,128)(2,1)S(1)} %get-tuple-element.127), channel_id=1, source_target_pairs={{0,1},{1,0},{2,3},{3,2},{4,5},{5,4},{6,7},{7,6},{8,9},{9,8},{10,11... | collective-permute-start | bytes 1474568 | tf_op jit(solution)/shard_map/ppermute | solution.py:44
  149.4 16.0 %collective-permute-start.45 = (bf16[384,640]{1,0:T(8,128)(2,1)S(1)}, bf16[384,640]{1,0:T(8,128)(2,1)S(1)}, u32[]{:S(2)}, u32[]{:S(2)}) collective-permute-start(bf16[384,640]{1,0:T(8,128)(2,1)S(1)} %get-tuple-element.128), channel_id=1, source_target_pairs={{0,2},{1,3},{2,0},{3,1},{4,6},{5,7},{6,4},{7,5},{8,10},{9,11},{10,... | collective-permute-start | bytes 1474568 | tf_op jit(solution)/shard_map/ppermute | solution.py:44
  161.6 18.1 %collective-permute-start.34 = (bf16[256,1408]{1,0:T(8,128)(2,1)}, bf16[256,1408]{1,0:T(8,128)(2,1)S(1)}, u32[]{:S(2)}, u32[]{:S(2)}) collective-permute-start(bf16[256,1408]{1,0:T(8,128)(2,1)} %get-tuple-element.98), channel_id=1, source_target_pairs={{0,16},{16,0},{1,17},{17,1},{2,18},{18,2},{3,19},{19,3},{4,20},{20... | collective-permute-start | bytes 2162696 | tf_op jit(solution)/shard_map/ppermute | solution.py:44
  163.1 18.1 %collective-permute-start.52 = (bf16[640,512]{1,0:T(8,128)(2,1)}, bf16[640,512]{1,0:T(8,128)(2,1)}, u32[]{:S(2)}, u32[]{:S(2)}) collective-permute-start(bf16[640,512]{1,0:T(8,128)(2,1)} %get-tuple-element.114), channel_id=1, source_target_pairs={{0,1},{1,0},{2,3},{3,2},{4,5},{5,4},{6,7},{7,6},{8,9},{9,8},{10,11... | collective-permute-start | bytes 1966088 | tf_op jit(solution)/shard_map/ppermute | solution.py:44
  163.8 17.3 %collective-permute-start.53 = (bf16[640,512]{1,0:T(8,128)(2,1)}, bf16[640,512]{1,0:T(8,128)(2,1)}, u32[]{:S(2)}, u32[]{:S(2)}) collective-permute-start(bf16[640,512]{1,0:T(8,128)(2,1)} %get-tuple-element.115), channel_id=1, source_target_pairs={{0,2},{1,3},{2,0},{3,1},{4,6},{5,7},{6,4},{7,5},{8,10},{9,11},{10,... | collective-permute-start | bytes 1966088 | tf_op jit(solution)/shard_map/ppermute | solution.py:44
  182.7 13.1 %collective-permute-start.54 = (bf16[320,512]{1,0:T(8,128)(2,1)S(1)}, bf16[320,512]{1,0:T(8,128)(2,1)S(1)}, u32[]{:S(2)}, u32[]{:S(2)}) collective-permute-start(bf16[320,512]{1,0:T(8,128)(2,1)S(1)} %dynamic-slice_convert_fusion), channel_id=1, source_target_pairs={{0,4},{4,0},{8,12},{12,8},{1,5},{5,1},{9,13},{13,9},{2,6},{6,2},{1... | collective-permute-start | bytes 983048 | tf_op jit(solution)/shard_map/ppermute | solution.py:44
  196.2 13.2 %collective-permute-start.55 = (bf16[160,512]{1,0:T(8,128)(2,1)S(1)}, bf16[160,512]{1,0:T(8,128)(2,1)S(1)}, u32[]{:S(2)}, u32[]{:S(2)}) collective-permute-start(bf16[160,512]{1,0:T(8,128)(2,1)S(1)} %dynamic-slice_convert_fusion.2), channel_id=1, source_target_pairs={{0,12},{4,8},{8,4},{12,0},{1,13},{5,9},{9,5},{13,1},{2,14},{6,10},... | collective-permute-start | bytes 491528 | tf_op jit(solution)/shard_map/ppermute | solution.py:44
  205.5 22.5 %collective-permute-start.50 = (bf16[384,640]{1,0:T(8,128)(2,1)S(1)}, bf16[384,640]{1,0:T(8,128)(2,1)S(1)}, u32[]{:S(2)}, u32[]{:S(2)}) collective-permute-start(bf16[384,640]{1,0:T(8,128)(2,1)S(1)} %maximum_select_fusion.4), channel_id=1, source_target_pairs={{0,16},{16,0},{1,17},{17,1},{2,18},{18,2},{3,19},{19,3},{4,20},{20... | collective-permute-start | bytes 1474568 | tf_op jit(solution)/shard_map/ppermute | solution.py:44
  213.9 13.4 %collective-permute-start.40 = (bf16[48,768]{1,0:T(8,128)(2,1)S(1)}, bf16[48,768]{1,0:T(8,128)(2,1)S(1)}, u32[]{:S(2)}, u32[]{:S(2)}) collective-permute-start(bf16[48,768]{1,0:T(8,128)(2,1)S(1)} %add_convert_fusion.2), channel_id=1, source_target_pairs={{0,12},{4,8},{8,4},{12,0},{1,13},{5,9},{9,5},{13,1},{2,14},{6,10},... | collective-permute-start | bytes 221192 | tf_op jit(solution)/shard_map/ppermute | solution.py:44
  217.9 17.1 %collective-permute-start.57 = (bf16[320,512]{1,0:T(8,128)(2,1)S(1)}, bf16[320,512]{1,0:T(8,128)(2,1)S(1)}, u32[]{:S(2)}, u32[]{:S(2)}) collective-permute-start(bf16[320,512]{1,0:T(8,128)(2,1)S(1)} %maximum_select_fusion.7), channel_id=1, source_target_pairs={{0,4},{4,0},{8,12},{12,8},{1,5},{5,1},{9,13},{13,9},{2,6},{6,2},{1... | collective-permute-start | bytes 983048 | tf_op jit(solution)/shard_map/ppermute | solution.py:44
  (123 other events, 951.4 us)
where the time goes:
time: 242 us; the launch traced here: 241 us
  waiting for transfers between devices  77.2 us (32%)
  starting transfers between devices  72 us (30%)
  local copies, waits for them, and re-layouts  37.7 us (16%)
  Pallas kernels  34.4 us (14%)
  other arithmetic  18.3 us (8%)
    ppermute x50, waiting for transfers between devices, swap(): return lax.ppermute(value, axis, [(i, i ^ flip) for i in range(size)])  60.9 us
    ppermute x50, starting transfers between devices, swap(): return lax.ppermute(value, axis, [(i, i ^ flip) for i in range(size)])  58.6 us
    pallas_call x9, Pallas kernels, kernel_call(): pl.pallas_call(body, out_shape=outs, in_specs=[pl.BlockSpec(memory_space=...  34.4 us
    unnamed x180, local copies, waits for them, and re-layouts  22.6 us
    ppermute x9, waiting for transfers between devices, swap_split(): return lax.ppermute(value, ('seq', axis), perm)  16.3 us
    ppermute x9, starting transfers between devices, swap_split(): return lax.ppermute(value, ('seq', axis), perm)  13.4 us
  transfers between devices with their start and end apart: 59, of which 21 were waited for; matrix products, arithmetic and copies ran while one was open for 11% of the time, Pallas kernels for 3%

commit v1 on v0

--- a/solution.py
+++ b/solution.py
@@ -54,27 +54,21 @@
     return lax.ppermute(value, ("seq", axis), perm)
 
 
-def gather4(value, core, axis, size, first, second):
-    one = swap(value, axis, first, size)
-    two = swap(value, axis, second, size)
-    both = swap_split(jnp.where(core == 0, one, two), axis, size, second, first)
-    return [value, one, two, both]
-
-
-def scatter4(blocks, core, axis, size, first, second):
-    via = swap_split(blocks[3], axis, size, second, first).astype(F32)
+def scatter4(blocks, via, core, axis, size, first, second, order):
+    via = via.astype(F32)
     none = jnp.zeros_like(via)
     one = (blocks[1].astype(F32) + jnp.where(core == 0, via, none)).astype(BF)
     two = (blocks[2].astype(F32) + jnp.where(core == 0, none, via)).astype(BF)
-    one = swap(one, axis, first, size).astype(F32)
-    two = swap(two, axis, second, size).astype(F32)
+    one = swap(order(one), axis, first, size).astype(F32)
+    two = swap(order(two), axis, second, size).astype(F32)
     return blocks[0].astype(F32) + one + two
 
 
 def halves(value, pick):
-    rows = value.shape[0] // 2
-    keep = lax.dynamic_slice_in_dim(value, pick * rows, rows, 0)
-    send = lax.dynamic_slice_in_dim(value, (1 - pick) * rows, rows, 0)
+    axis = value.ndim - 2
+    rows = value.shape[axis] // 2
+    keep = lax.dynamic_slice_in_dim(value, pick * rows, rows, axis)
+    send = lax.dynamic_slice_in_dim(value, (1 - pick) * rows, rows, axis)
     return keep, send
 
 
@@ -84,21 +78,71 @@
     )
 
 
-def ctx_sum(value, size, order):
-    if size != 4:
-        return lax.psum(value.astype(BF), "ctx")
+class Order:
+    def __init__(self):
+        self.last = None
+
+    def __call__(self, value):
+        if self.last is not None:
+            value = lax.optimization_barrier((value, self.last))[0]
+        self.last = value
+        return value
+
+    def wait(self, value):
+        return lax.optimization_barrier((value, self.last))[0]
+
+
+def reduce_steps(blocks, core, ctx_size, cuts, order):
     place = lax.axis_index("ctx")
     high = place // 2
     odd = lax.rem(place, 2)
     mixed = lax.rem(high + odd, 2)
-    steps = [(1, mixed), (3, high)] if order == 0 else [(3, high), (1, mixed)]
-    for flip, pick in steps:
-        keep, send = halves(value, pick)
-        value = keep.astype(F32) + swap(send.astype(BF), "ctx", flip, 4).astype(F32)
-    value = value.astype(BF)
-    for flip, pick in steps[::-1]:
-        value = join(value, swap(value, "ctx", flip, 4), pick)
-    return value
+    steps = [(1, mixed), (3, high)]
+    via = swap_split(order(blocks[3]), "fsdp", 4, 2, 1)
+    yield
+    via = order.wait(via).astype(F32)
+    none = jnp.zeros_like(via)
+    one = (blocks[1].astype(F32) + jnp.where(core == 0, via, none)).astype(BF)
+    two = (blocks[2].astype(F32) + jnp.where(core == 0, none, via)).astype(BF)
+    one = swap(order(one), "fsdp", 1, 4)
+    two = swap(order(two), "fsdp", 2, 4)
+    yield
+    one, two = order.wait(one), order.wait(two)
+    value = blocks[0].astype(F32) + one.astype(F32) + two.astype(F32)
+    if ctx_size != 4:
+        value = lax.psum(value.astype(BF), "ctx")
+    elif not cuts:
+        for flip in (1, 3):
+            value = value.astype(BF)
+            got = swap(order(value), "ctx", flip, 4)
+            yield
+            value = value.astype(F32) + order.wait(got).astype(F32)
+        value = value.astype(BF)
+    pieces = [value]
+    if cuts:
+        edges = [0, *cuts, value.shape[1]]
+        pieces = [value[:, a:b] for a, b in zip(edges, edges[1:])]
+    if cuts and ctx_size == 4:
+        turns = [steps, steps[::-1]]
+        for k in range(2):
+            got, keep = [], []
+            for piece, turn in zip(pieces, turns):
+                flip, pick = turn[k]
+                kept, send = halves(piece, pick)
+                keep.append(kept)
+                got.append(swap(order(send.astype(BF)), "ctx", flip, 4))
+            yield
+            pieces = [a.astype(F32) + order.wait(b).astype(F32) for a, b in zip(keep, got)]
+        pieces = [piece.astype(BF) for piece in pieces]
+        for k in (1, 0):
+            got = [swap(order(p), "ctx", turn[k][0], 4) for p, turn in zip(pieces, turns)]
+            yield
+            pieces = [
+                join(p, order.wait(b), turn[k][1]) for p, b, turn in zip(pieces, got, turns)
+            ]
+    others = [swap_pair(order(piece)) for piece in pieces]
+    yield
+    yield pieces, others
 
 
 def attend_forward(queries, key_rows, values, query_order, key_order, score_scale):
@@ -139,19 +183,72 @@
     return (jnp.stack(query_grads, axis=1), key_grad, value_grad)
 
 
-def kernel_call(body, outs, args, flops, scratch=(), smem=()):
+class Waiting:
+    def __init__(self, ref, copy):
+        self.ref, self.copy = ref, copy
+
+    def wait(self):
+        if self.copy is not None:
+            self.copy.wait()
+            self.copy = None
+
+    def __getitem__(self, index):
+        self.wait()
+        return self.ref[index]
+
+
+def kernel_call(body, outs, args, flops, scratch=(), smem=(), far=(), back=(), room=16, flushes=0):
     nbytes = sum(a.size * a.dtype.itemsize for a in args)
     nbytes += sum(o.size * o.dtype.itemsize for o in outs)
-    vmem = pl.BlockSpec(memory_space=pltpu.VMEM)
+    hbm = pl.BlockSpec(memory_space=pltpu.HBM)
+    specs = {i: hbm for i in far}
+    specs.update({i: pl.BlockSpec(memory_space=pltpu.SMEM) for i in smem})
+    n_in, n_out, n_own = len(args), len(outs), len(scratch)
+
+    def wrapped(*refs):
+        ins, dests = list(refs[:n_in]), list(refs[n_in : n_in + n_out])
+        rest = refs[n_in + n_out :]
+        own, rest = rest[:n_own], rest[n_own:]
+        sems = rest[-1]
+        for k, i in enumerate(far):
+            copy = pltpu.make_async_copy(ins[i], rest[k], sems.at[k])
+            copy.start()
+            ins[i] = Waiting(rest[k], copy)
+        kept = list(dests)
+        for k, i in enumerate(back):
+            kept[i] = rest[len(far) + k]
+        copies = []
+        flushed = set()
+
+        def flush(which, cols):
+            at = (slice(None), cols)
+            sem = sems.at[len(far) + len(back) + len(copies)]
+            copies.append(pltpu.make_async_copy(kept[which].at[at], dests[which].at[at], sem))
+            copies[-1].start()
+            flushed.add(which)
+
+        body(*ins, *kept, *own, *([flush] if flushes else []))
+        for k, i in enumerate(back):
+            if i in flushed:
+                continue
+            copies.append(pltpu.make_async_copy(kept[i], dests[i], sems.at[len(far) + k]))
+            copies[-1].start()
+        for i in far:
+            ins[i].wait()
+        for copy in copies:
+            copy.wait()
+
+    buffers = [pltpu.VMEM(args[i].shape, args[i].dtype) for i in far]
+    buffers += [pltpu.VMEM(outs[i].shape, outs[i].dtype) for i in back]
     return pl.pallas_call(
-        body,
+        wrapped,
         out_shape=outs,
-        in_specs=[
-            pl.BlockSpec(memory_space=pltpu.SMEM) if i in smem else vmem for i in range(len(args))
-        ],
-        out_specs=[vmem] * len(outs),
-        scratch_shapes=list(scratch),
-        compiler_params=pltpu.CompilerParams(vmem_limit_bytes=48 * 1024 * 1024),
+        in_specs=[specs.get(i, pl.BlockSpec()) for i in range(n_in)],
+        out_specs=[hbm if i in back else pl.BlockSpec() for i in range(n_out)],
+        scratch_shapes=list(scratch)
+        + buffers
+        + [pltpu.SemaphoreType.DMA((max(1, len(far) + len(back) + flushes),))],
+        compiler_params=pltpu.CompilerParams(vmem_limit_bytes=room * 1024 * 1024),
         cost_estimate=pl.CostEstimate(flops=flops, bytes_accessed=nbytes, transcendentals=0),
     )(*args)
 
@@ -176,65 +273,108 @@
     return pl.ds(pl.multiple_of(start, step), size)
 
 
-def key_value(inputs, blocks, norm_in, norm_key, cosine, sine, block_ids):
+def pack(w_query, w_key, w_value, gains):
+    rows = w_query.shape[0] // 2
+    widths = [w.shape[1] for w in (w_query, w_key, w_value)]
+    total = sum(widths)
+
+    def body(*refs):
+        weights, (mine, other) = refs[:3], refs[-2:]
+        core = lax.axis_index("seq")
+        start = 0
+        for ref, width in zip(weights, widths):
+            at = slice(start, start + width)
+            low, high = ref[:rows, :], ref[rows:, :]
+            mine[:rows, at] = jnp.where(core == 0, low, high)
+            other[:, at] = jnp.where(core == 0, high, low)
+            start += width
+        mine[rows:, :] = jnp.zeros((16, total), BF)
+        for number, (ref, gain) in enumerate(zip(refs[3:-2], gains)):
+            row = ref[...].astype(F32).reshape(1, gain.shape[0])
+            mine[rows + number : rows + number + 1, : gain.shape[0]] = row.astype(BF)
+
+    outs = [shape((rows + 16, total), BF), shape((rows, total), BF)]
+    args = [w_query, w_key, w_value, *gains]
+    return kernel_call(body, outs, args, 0, room=62)
+
+
+def pack_ffn(w_gate, w_up, w_down, w_out):
+    width = w_gate.shape[0]
+    sizes = [w_gate.shape[1] // 2, w_up.shape[1] // 2, w_down.shape[0] // 2, w_out.shape[0] // 2]
+    total = sum(sizes)
+
+    def body(gate, up, down, out, mine, other):
+        core = lax.axis_index("seq")
+        start = 0
+        for ref, size, turn in zip((gate, up, down, out), sizes, (False, False, True, True)):
+            at = slice(start, start + size)
+            low = ref[:size, :].T if turn else ref[:, :size]
+            high = ref[size:, :].T if turn else ref[:, size:]
+            mine[:, at] = jnp.where(core == 0, low, high)
+            other[:, at] = jnp.where(core == 0, high, low)
+            start += size
+
+    outs = [shape((width, total), BF)] * 2
+    args = [w_gate, w_up, w_down, w_out]
+    return kernel_call(body, outs, args, 0, room=62), sizes[0]
+
+
+def project(inputs, mine, other, size, cosine, sine, block_ids):
     rows, width = inputs.shape
-    size = norm_key.shape[1]
-    shard = width // 4
-
-    def body(x, w0, w1, w2, w3, g_in, g_key, cos, sin, ids, hidden, key_pre, packed, full):
+    part, total = other[0].shape
+    cols = total - 2 * size
+    heads = cols // size
+
+    def body(x, *refs):
+        blocks, refs = refs[:8], refs[8:]
+        cos, sin, ids = refs[:3]
+        hidden, key_pre, packed, query_pre, queries, full, wide, narrow = refs[3:]
         place = lax.axis_index("fsdp")
-        for flip, block in enumerate((w0, w1, w2, w3)):
-            full[rows_at((place ^ flip) * shard, shard, 16), :] = block[:shard, :]
+        core = lax.axis_index("seq")
+        for flip in range(4):
+            start = (place ^ flip) * 2
+            full[rows_at((start + core) * part, part, 16), :] = blocks[flip][:part, :]
+            full[rows_at((start + 1 - core) * part, part, 16), :] = blocks[4 + flip][:part, :]
+        rows_of = [blocks[flip][part:, : width // 4].astype(F32) for flip in range(4)]
+        for index in range(4):
+            piece = rows_of[0]
+            for flip in range(1, 4):
+                piece = jnp.where((place ^ flip) == index, rows_of[flip], piece)
+            wide[:, index * (width // 4) : (index + 1) * (width // 4)] = piece
+            narrow[:, index * (size // 4) : (index + 1) * (size // 4)] = piece[:, : size // 4]
+        g_in, g_query, g_key = wide[0:1, :], narrow[4:5, :], narrow[5:6, :]
         value = x[...].astype(F32)
-        hid = (value * rms_scale(value) * g_in[...]).astype(BF)
+        hid = (value * rms_scale(value) * g_in).astype(BF)
         hidden[...] = hid
-        both = matmul(hid, full[...])
+        both = matmul(hid, full[:, cols:])
         key = both[:, :size]
         key_pre[...] = key
-        turned = rotate(key * rms_scale(key) * g_key[...], cos[...], sin[...])
+        turned = rotate(key * rms_scale(key) * g_key, cos[...], sin[...])
         packed[:rows, :size] = turned.astype(BF)
         packed[:rows, size:] = both[:, size:].astype(BF)
         row = lax.broadcasted_iota(jnp.int32, (16, 2 * size), 0)
         packed[rows:, :] = jnp.where(row == 0, ids[0, 0], ids[0, 1]).astype(F32).astype(BF)
+        for head in range(heads):
+            at = slice(head * size, (head + 1) * size)
+            value = matmul(hid, full[:, at])
+            query_pre[:, at] = value
+            turned = rotate(value * rms_scale(value) * g_query, cos[...], sin[...])
+            queries[head] = turned.astype(BF)
 
     outs = [
         shape((rows, width), BF),
         shape((rows, size), F32),
         shape((rows + 16, 2 * size), BF),
-        shape((width, 2 * size), BF),
-    ]
-    args = [inputs, *blocks, norm_in, norm_key, cosine, sine, block_ids]
-    return kernel_call(body, outs, args, 4 * rows * width * size, smem=(9,))
-
-
-def query(hidden, mine, other, norm_query, cosine, sine):
-    rows, width = hidden.shape
-    size = norm_query.shape[1]
-    part, cols = mine[0].shape
-    heads = cols // size
-
-    def body(hid, *refs):
-        blocks, (g_query, cos, sin, query_pre, queries, full) = refs[:8], refs[8:]
-        place = lax.axis_index("fsdp")
-        core = lax.axis_index("seq")
-        for flip in range(4):
-            start = (place ^ flip) * 2
-            full[rows_at((start + core) * part, part, 16), :] = blocks[flip][...]
-            full[rows_at((start + 1 - core) * part, part, 16), :] = blocks[4 + flip][...]
-        for head in range(heads):
-            at = slice(head * size, (head + 1) * size)
-            value = matmul(hid[...], full[:, at])
-            query_pre[:, at] = value
-            turned = rotate(value * rms_scale(value) * g_query[...], cos[...], sin[...])
-            queries[head] = turned.astype(BF)
-
-    outs = [
         shape((rows, cols), F32),
         shape((heads, rows, size), BF),
-        shape((width, cols), BF),
+        shape((width, total), BF),
+        shape((16, width), F32),
+        shape((16, size), F32),
     ]
-    args = [hidden, *mine, *other, norm_query, cosine, sine]
-    return kernel_call(body, outs, args, 2 * rows * width * cols)
+    args = [inputs, *mine, *other, cosine, sine, block_ids]
+    flops = 2 * rows * width * total
+    far = (0, 9, 10)
+    return kernel_call(body, outs, args, flops, smem=(11,), far=far, back=(0, 1, 3, 5), room=62)
 
 
 def tile_masks(blocks, rows):
@@ -279,16 +419,39 @@
             logsum[head] = highest + jnp.log(summed)
 
     outs = [shape((heads, rows, size), BF), shape((heads, rows, 1), F32)]
-    return kernel_call(body, outs, [queries, *kv_blocks], 4 * heads * rows * rows * count * size)
-
-
-def attend_back_kernel(queries, kv_blocks, logsum, out_grad, score_scale):
+    flops = 4 * heads * rows * rows * count * size
+    far = tuple(range(1, 1 + count))
+    return kernel_call(body, outs, [queries, *kv_blocks], flops, far=far, room=24)
+
+
+def query_head_back(grad, value, gain, cosine, sine):
+    turned = rotate(grad, cosine, -sine)
+    back, gain_grad = rms_back(value, rms_scale(value), gain, turned)
+    return back.astype(BF), gain_grad
+
+
+def split_heads(parts, core, mine, other, size):
+    per = len(parts) // 2
+    for head in range(per):
+        at = slice(head * size, (head + 1) * size)
+        mine[:, at] = jnp.where(core == 0, parts[head], parts[per + head])
+        other[:, at] = jnp.where(core == 0, parts[per + head], parts[head])
+
+
+def attend_back_kernel(
+    queries, kv_blocks, logsum, out_grad, score_scale, query_pre, norm_query, cosine, sine, full
+):
     heads, rows, size = queries.shape
+    width = full.shape[0]
+    per = heads // 2
     count = len(kv_blocks)
 
     def body(*refs):
         q, blocks, refs = refs[0], refs[1 : 1 + count], refs[1 + count :]
-        lse, grads, query_grad, kv_grads, kv_acc = refs[0], refs[1], refs[2], refs[3:-1], refs[-1]
+        lse, grads, pre, g_query, cos, sin, full = refs[:7]
+        kv_grads, (hidden_part, mine, other, gain_grad, kv_acc) = refs[7 : 7 + count], refs[7 + count :]
+        core = lax.axis_index("seq")
+        query_grads, gains, hidden = [], None, None
         masks = tile_masks(blocks, rows)
         for head in range(heads):
             q_head, g_head = q[head], grads[head]
@@ -317,17 +480,37 @@
                 else:
                     kv_acc[i, :, :size] += key_part
                     kv_acc[i, :, size:] += value_part
-            query_grad[head] = total * score_scale
+            at = slice(head * size, (head + 1) * size)
+            back, gain = query_head_back(
+                total * score_scale, pre[:, at], g_query[4:5, :], cos[...], sin[...]
+            )
+            query_grads.append(back)
+            gains = gain if gains is None else gains + gain
+            part = inner_cols(back, full[:, at])
+            hidden = part if hidden is None else hidden + part
         for i in range(count):
             kv_grads[i][...] = kv_acc[i].astype(BF)
-
-    outs = [shape((heads, rows, size), F32)] + [shape((rows, 2 * size), BF)] * count
+        hidden_part[...] = hidden
+        split_heads(query_grads, core, mine, other, size)
+        gain_grad[...] = gains
+
+    outs = [shape((rows, 2 * size), BF)] * count + [
+        shape((rows, width), F32),
+        shape((rows, per * size), BF),
+        shape((rows, per * size), BF),
+        shape((1, size), F32),
+    ]
     return kernel_call(
         body,
         outs,
-        [queries, *kv_blocks, logsum, out_grad],
+        [
+            queries, *kv_blocks, logsum, out_grad, query_pre, norm_query, cosine, sine, full,
+        ],
         10 * heads * rows * rows * count * size,
         scratch=[pltpu.VMEM((count, rows, 2 * size), F32)],
+        far=tuple(range(2 + count)) + tuple(k + count for k in (3, 5, 6, 7)),
+        back=tuple(range(3 + count)),
+        room=62,
     )
 
 
@@ -341,36 +524,37 @@
 
 
 def feed_forward(
-    inputs, cotangent, context, out_mine, out_other, gate_up, down, norm_attn, norm_pre, norm_post
+    inputs, cotangent, context, blocks, unit, wide_gains
 ):
     heads, rows, size = context.shape
     width = inputs.shape[1]
-    unit = down[0].shape[0]
     half = size // 2
-    count = len(down)
+    count = len(blocks)
     hidden = unit * count // 2
     offs = [0, width, 2 * width, 3 * width]
     offs += [offs[3] + hidden, offs[3] + 2 * hidden, offs[3] + 3 * hidden]
     total_cols = offs[6] + heads * half
 
     def body(x, cot, ctx, *refs):
-        om, oo, gu, dn = refs[:4], refs[4:8], refs[8 : 8 + count], refs[8 + count : 8 + 2 * count]
-        refs = refs[8 + 2 * count :]
-        g_attn, g_pre, g_post = refs[0][...], refs[1][...], refs[2][...]
-        result, middle_grad, own, send, ctx_grad, gain_grads = refs[3:9]
-        w_out, gate, up = refs[9:]
+        blocks, refs = refs[:count], refs[count:]
+        gate_at, up_at = slice(0, unit), slice(unit, 2 * unit)
+        both_at, down_at, out_at = slice(0, 2 * unit), slice(2 * unit, 3 * unit), slice(3 * unit, None)
+        g_attn, g_pre, g_post = [refs[0][k : k + 1, :] for k in (1, 2, 3)]
+        result, middle_grad, own, send, ctx_grad, gain_grads = refs[1:7]
+        w_out, gate, up, flush = refs[7:]
         place = lax.axis_index("fsdp")
         core = lax.axis_index("seq")
         attn_out = None
         for flip in range(4):
-            w_out[flip, rows_at(core * half, half, 16), :] = om[flip][...]
-            w_out[flip, rows_at((1 - core) * half, half, 16), :] = oo[flip][...]
+            a, b = blocks[flip][:, out_at], blocks[4 + flip][:, out_at]
+            w_out[flip, :, :half] = jnp.where(core == 0, a, b)
+            w_out[flip, :, half:] = jnp.where(core == 0, b, a)
             value = ctx[place ^ flip]
             low, high = value[:, :half], value[:, half:]
             at = slice(offs[6] + flip * half, offs[6] + (flip + 1) * half)
             own[:, at] = jnp.where(core == 0, low, high)
             send[:, at] = jnp.where(core == 0, high, low)
-            part = matmul(value, w_out[flip])
+            part = inner_cols(value, w_out[flip])
             attn_out = part if attn_out is None else attn_out + part
         inv_attn = rms_scale(attn_out)
         middle = x[...].astype(F32) + attn_out * inv_attn * g_attn
@@ -380,18 +564,23 @@
         send[:, : offs[1]] = ffn_in
         ffn_out = None
         for i in range(count):
-            pre = matmul(ffn_in, gu[i][...])
-            gate_pre, up_pre = pre[:, :unit], pre[:, unit:]
-            gate[i] = gate_pre
-            up[i] = up_pre
-            mixed = (gelu_parts(gate_pre)[0] * up_pre).astype(BF)
+            pre = matmul(ffn_in, blocks[i][:, both_at])
+            activated, slope = gelu_parts(pre[:, :unit])
+            up_pre = pre[:, unit:]
+            gate[i] = up_pre * slope
+            up[i] = activated
+            mixed = (activated * up_pre).astype(BF)
             j = i % (count // 2)
             dest = own if i < count // 2 else send
             dest[:, offs[3] + j * unit : offs[3] + (j + 1) * unit] = mixed
-            part = matmul(mixed, dn[i][...])
+            part = inner_cols(mixed, blocks[i][:, down_at])
             ffn_out = part if ffn_out is None else ffn_out + part
         inv_post = rms_scale(ffn_out)
         result[...] = middle + ffn_out * inv_post * g_post
+        flush(0, slice(0, width))
+        for k in (2, 3):
+            flush(k, slice(offs[3], offs[4]))
+            flush(k, slice(offs[6], total_cols))
         grad = cot[...].astype(F32)
         ffn_grad, post_grad = rms_back(ffn_out, inv_post, g_post, grad)
         ffn_grad = ffn_grad.astype(BF)
@@ -399,16 +588,19 @@
         send[:, offs[1] : offs[2]] = ffn_grad
         pre_total = None
         for i in range(count):
-            mixed_grad = inner_cols(ffn_grad, dn[i][...])
-            activated, slope = gelu_parts(gate[i])
-            gate_grad = (mixed_grad * up[i] * slope).astype(BF)
-            up_grad = (mixed_grad * activated).astype(BF)
+            mixed_grad = matmul(ffn_grad, blocks[i][:, down_at])
+            gate_grad = (mixed_grad * gate[i]).astype(BF)
+            up_grad = (mixed_grad * up[i]).astype(BF)
             j = i % (count // 2)
             dest = own if i < count // 2 else send
             dest[:, offs[4] + j * unit : offs[4] + (j + 1) * unit] = gate_grad
             dest[:, offs[5] + j * unit : offs[5] + (j + 1) * unit] = up_grad
-            part = inner_cols(gate_grad, gu[i][:, :unit]) + inner_cols(up_grad, gu[i][:, unit:])
+            part = inner_cols(gate_grad, blocks[i][:, gate_at])
+            part = part + inner_cols(up_grad, blocks[i][:, up_at])
             pre_total = part if pre_total is None else pre_total + part
+        for k in (2, 3):
+            flush(k, slice(offs[4], offs[6]))
+            flush(k, slice(0, offs[2]))
         part, pre_grad = rms_back(middle, inv_pre, g_pre, pre_total)
         mid_grad = grad + part
         middle_grad[...] = mid_grad
@@ -416,8 +608,10 @@
         attn_grad = attn_grad.astype(BF)
         own[:, offs[2] : offs[3]] = attn_grad
         send[:, offs[2] : offs[3]] = attn_grad
+        for k in (2, 3):
+            flush(k, slice(offs[2], offs[3]))
         for flip in range(4):
-            ctx_grad[place ^ flip] = inner_cols(attn_grad, w_out[flip]).astype(BF)
+            ctx_grad[place ^ flip] = matmul(attn_grad, w_out[flip]).astype(BF)
         gain_grads[...] = jnp.concatenate(
             [attn_gain, pre_grad, post_grad, jnp.zeros((5, width), F32)], 0
         )
@@ -430,15 +624,17 @@
         shape((heads, rows, size), BF),
         shape((8, width), F32),
     ]
-    args = [inputs, cotangent, context, *out_mine, *out_other, *gate_up, *down]
-    args += [norm_attn, norm_pre, norm_post]
+    args = [inputs, cotangent, context, *blocks]
+    args += [wide_gains]
     scratch = [
-        pltpu.VMEM((4, size, width), BF),
+        pltpu.VMEM((4, width, size), BF),
         pltpu.VMEM((count, rows, unit), F32),
         pltpu.VMEM((count, rows, unit), F32),
     ]
     flops = 2 * rows * width * (6 * unit * count + 2 * heads * size)
-    return kernel_call(body, outs, args, flops, scratch), offs
+    far = (0, 1) + tuple(range(3, 3 + count))
+    back = (0, 1, 2, 3, 5)
+    return kernel_call(body, outs, args, flops, scratch, far=far, back=back, room=48, flushes=11), offs
 
 
 def ffn_weight_grads(own, got, offs, unit, half):
@@ -453,16 +649,15 @@
 
         at = lambda k, j, size: slice(offs[k] + j * size, offs[k] + (j + 1) * size)
         whole = lambda k: slice(offs[k], offs[k] + width)
-        for j in range(4):
-            rest, gate_up = outs[j], outs[4 + j]
-            rest[:unit, :] = product(at(3, j, unit), whole(1))
-            rest[unit:, :] = product(at(6, j, half), whole(2))
-            gate_up[:, :unit] = product(whole(0), at(4, j, unit))
-            gate_up[:, unit:] = product(whole(0), at(5, j, unit))
-
-    outs = [shape((unit + half, width), BF)] * 4 + [shape((width, 2 * unit), BF)] * 4
+        for j, out in enumerate(outs):
+            out[:, :unit] = product(whole(0), at(4, j, unit))
+            out[:, unit : 2 * unit] = product(whole(0), at(5, j, unit))
+            out[:, 2 * unit : 3 * unit] = product(whole(1), at(3, j, unit))
+            out[:, 3 * unit :] = product(whole(2), at(6, j, half))
+
+    outs = [shape((width, 3 * unit + half), BF)] * 4
     flops = 4 * rows * width * 4 * (3 * unit + half)
-    return kernel_call(body, outs, [own, got], flops)
+    return kernel_call(body, outs, [own, got], flops, far=(0, 1), back=tuple(range(4)), room=62)
 
 
 def query_back(query_grad, query_pre, norm_query, cosine, sine, query_full):
@@ -472,23 +667,16 @@
 
     def body(grad, pre, g_query, cos, sin, full, hidden_part, mine, other, gain_grad):
         core = lax.axis_index("seq")
-        gains = None
-        outs = []
-        total = None
+        gains, parts, total = None, [], None
         for head in range(heads):
             at = slice(head * size, (head + 1) * size)
-            value = pre[:, at]
-            turned = rotate(grad[head], cos[...], -sin[...])
-            back, gain = rms_back(value, rms_scale(value), g_query[...], turned)
+            back, gain = query_head_back(grad[head], pre[:, at], g_query[4:5, :], cos[...], sin[...])
             gains = gain if gains is None else gains + gain
-            outs.append(back.astype(BF))
-            part = inner_cols(outs[-1], full[:, at])
+            parts.append(back)
+            part = inner_cols(back, full[:, at])
             total = part if total is None else total + part
         hidden_part[...] = total
-        for head in range(per):
-            at = slice(head * size, (head + 1) * size)
-            mine[:, at] = jnp.where(core == 0, outs[head], outs[per + head])
-            other[:, at] = jnp.where(core == 0, outs[per + head], outs[head])
+        split_heads(parts, core, mine, other, size)
         gain_grad[...] = gains
 
     outs = [
@@ -498,7 +686,8 @@
         shape((1, size), F32),
     ]
     args = [query_grad, query_pre, norm_query, cosine, sine, query_full]
-    return kernel_call(body, outs, args, 2 * rows * width * heads * size)
+    flops = 2 * rows * width * heads * size
+    return kernel_call(body, outs, args, flops, far=(1, 3, 4, 5), back=(0, 1, 2), room=24)
 
 
 def input_back(
@@ -517,14 +706,15 @@
         core = lax.axis_index("seq")
         value = k_pre[...]
         turned = rotate(back[:, :size], cos[...], -sin[...])
-        key_grad, gain = rms_back(value, rms_scale(value), g_key[...], turned)
+        key_grad, gain = rms_back(value, rms_scale(value), g_key[5:6, :], turned)
         key_gain[...] = gain
         key_grad = key_grad.astype(BF)
         value_grad = back[:, size:].astype(BF)
-        total = part[...] + inner_cols(key_grad, full[:, :size])
-        total = total + inner_cols(value_grad, full[:, size:])
+        at = 2 * per
+        total = part[...] + inner_cols(key_grad, full[:, at : at + size])
+        total = total + inner_cols(value_grad, full[:, at + size :])
         value = x[...].astype(F32)
-        grad, gain = rms_back(value, rms_scale(value), g_in[...], total)
+        grad, gain = rms_back(value, rms_scale(value), g_in[0:1, :], total)
         input_grad[...] = mid[...] + grad
         in_gain[...] = gain
         own[:, :width] = hid[...]
@@ -543,7 +733,9 @@
     ]
     args = [kv_back, key_pre, norm_key, cosine, sine, kv_full, hidden_part, inputs, norm_in]
     args += [middle_grad, hidden, query_mine, query_other]
-    return kernel_call(body, outs, args, 4 * rows * width * size)
+    flops = 4 * rows * width * size
+    far = (1, 3, 4, 5, 6, 7, 9, 10, 11, 12)
+    return kernel_call(body, outs, args, flops, far=far, back=(0, 1, 2), room=24)
 
 
 def late_grads(own, got, gains, width):
@@ -562,7 +754,9 @@
     outs = [shape((shard + gains.shape[1], out_cols), BF)] * 4
     flops = 4 * rows * width * out_cols
     scratch = [pltpu.VMEM((width, out_cols), F32)]
-    return kernel_call(body, outs, [own, got, gains], flops, scratch)
+    return kernel_call(
+        body, outs, [own, got, gains], flops, scratch, far=(0, 1), back=tuple(range(4))
+    )
 
 
 def pick_half(value, which, axis):
@@ -610,59 +804,26 @@
 
         gains = [gain_in, gain_attn, gain_pre, gain_post, gain_query, gain_key]
         gain_sizes = [member.shape[0] for member in gains]
-        kv_width = 2 * head_size
         shard_rows = w_key.shape[0]
-        gain_row = jnp.concatenate(gains)
-        gain_row = jnp.pad(gain_row, (0, 16 * kv_width - gain_row.shape[0]))
-        packed = jnp.concatenate(
-            [jnp.concatenate([w_key, w_value], 1), gain_row.reshape(16, kv_width)], 0
-        )
+        packed, packed_other = pack(w_query, w_key, w_value, gains)
         first = [packed] + [swap(packed, "fsdp", flip, 4) for flip in (1, 2, 3)]
-        used = -(-sum(gain_sizes) // kv_width)
-        rows = [block[shard_rows : shard_rows + used].astype(F32) for block in first]
-        placed = []
-        for index in range(4):
-            row = rows[0]
-            for flip in range(1, 4):
-                row = jnp.where((fsdp ^ flip) == index, rows[flip], row)
-            placed.append(row.reshape(-1))
-        placed = jnp.stack(placed, 0)
-        norms = []
-        start = 0
-        for size in gain_sizes:
-            norms.append(placed[:, start : start + size].reshape(1, -1))
-            start += size
-        norm_in, norm_attn, norm_pre, norm_post, norm_query, norm_key = norms
-
-        def fetch(mine, other):
-            mine = gather4(mine, core, "fsdp", 4, 1, 2)
-            return mine, [other] + [swap_pair(block) for block in mine[1:]]
-
-        def fetch_half(shard, *order):
-            mine, other = pick_half(shard, core, 0), pick_half(shard, 1 - core, 0)
-            return fetch(after(mine, *order), other)
-
-        query_mine, query_other = fetch_half(w_query, first[3])
-        out_mine, out_other = fetch_half(w_out, query_mine[1], query_mine[2])
-        gate_up = jnp.concatenate([pick_half(w_gate, core, 1), pick_half(w_up, core, 1)], 1)
-        gate_up_other = jnp.concatenate(
-            [pick_half(w_gate, 1 - core, 1), pick_half(w_up, 1 - core, 1)], 1
-        )
-        gu_mine, gu_other = fetch(after(gate_up, out_mine[1], out_mine[2]), gate_up_other)
-        down_mine, down_other = fetch_half(w_down, gu_mine[1], gu_mine[2])
-        unit = gate_up.shape[1] // 2
+        first_other = [packed_other] + [swap_pair(block) for block in first[1:]]
+        (ffn_mine, ffn_other), unit = pack_ffn(w_gate, w_up, w_down, w_out)
+        sent = after(ffn_mine, *first[1:])
+        ffn_one = swap(sent, "fsdp", 1, 4)
+        ffn_two = swap(sent, "fsdp", 2, 4)
 
         cosine, sine = tables(positions[0], head_size)
-        hidden, key_pre, packed_kv, kv_full = key_value(
-            inputs, first, norm_in, norm_key, cosine, sine, block_ids
+        hidden, key_pre, packed_kv, query_pre, queries, qkv_full, wide_gains, narrow_gains = project(
+            inputs, first, first_other, head_size, cosine, sine, block_ids
         )
         if ctx_size == 4:
-            kv_blocks = gather4(packed_kv, core, "ctx", 4, 1, 3)
+            kv_one, kv_two = swap(packed_kv, "ctx", 1, 4), swap(packed_kv, "ctx", 3, 4)
+            sent = jnp.where(core == 0, kv_one, kv_two)
+            ffn_one, ffn_two, sent = lax.optimization_barrier((ffn_one, ffn_two, sent))
+            kv_blocks = [packed_kv, kv_one, kv_two, swap_split(sent, "ctx", 4, 3, 1)]
         else:
             kv_all = lax.all_gather(packed_kv, "ctx", axis=0)
-        query_pre, queries, query_full = query(
-            hidden, query_mine, query_other, norm_query, cosine, sine
-        )
         if ctx_size == 4:
             context, logsum = attend_kernel(queries, kv_blocks, score_scale)
         else:
@@ -678,35 +839,39 @@
             )
             context = seq_out.astype(BF).transpose(1, 0, 2)
 
+        ffn_opposite = swap_split(jnp.where(core == 0, ffn_one, ffn_two), "fsdp", 4, 2, 1)
+        ffn_blocks = [ffn_mine, ffn_one, ffn_two, after(ffn_opposite, context)]
+        ffn_blocks += [ffn_other] + [swap_pair(block) for block in ffn_blocks[1:]]
+
         (result, middle_grad, own, send, context_grad, gain_grads), offs = feed_forward(
             inputs,
             cotangent,
             context,
-            out_mine,
-            out_other,
-            gu_mine + gu_other,
-            down_mine + down_other,
-            norm_attn,
-            norm_pre,
-            norm_post,
+            ffn_blocks,
+            unit,
+            wide_gains,
         )
 
         parts = ffn_weight_grads(own, swap_pair(send), offs, unit, head_size // 2)
-        rest_sum = ctx_sum(scatter4(parts[:4], core, "fsdp", 4, 1, 2), ctx_size, 1)
-        gu_sum = ctx_sum(scatter4(parts[4:], core, "fsdp", 4, 1, 2), ctx_size, 0)
-        rest_other = swap_pair(rest_sum)
-        gu_other = swap_pair(gu_sum)
-        total_down = join(rest_sum[:unit], rest_other[:unit], core).astype(F32)
-        total_out = join(rest_sum[unit:], rest_other[unit:], core).astype(F32)
-        total_gate = join_cols(gu_sum[:, :unit], gu_other[:, :unit], core)
-        total_up = join_cols(gu_sum[:, unit:], gu_other[:, unit:], core)
-
-        context_grad = after(context_grad, *parts)
+        order = Order()
+        ffn_steps = reduce_steps(parts, core, ctx_size, (2 * unit,), order)
+        next(ffn_steps)
+        context_grad = after(context_grad, parts[0])
+
         if ctx_size == 4:
-            query_grad, *kv_parts = attend_back_kernel(
-                queries, kv_blocks, logsum, context_grad, score_scale
+            *kv_parts, hidden_part, back_mine, back_other, grad_query = attend_back_kernel(
+                queries,
+                kv_blocks,
+                logsum,
+                context_grad,
+                score_scale,
+                query_pre,
+                narrow_gains,
+                cosine,
+                sine,
+                qkv_full,
             )
-            kv_back = scatter4(kv_parts, core, "ctx", 4, 1, 3)
+            kv_via = swap_split(kv_parts[3], "ctx", 4, 3, 1)
         else:
             query_grad, key_grad, value_grad = attend_backward(
                 by_row,
@@ -720,20 +885,24 @@
             )
             query_grad = query_grad.transpose(1, 0, 2)
             kv_grad = jnp.concatenate([key_grad, value_grad], 1).astype(BF)
+            hidden_part, back_mine, back_other, grad_query = query_back(
+                query_grad, query_pre, narrow_gains, cosine, sine, qkv_full
+            )
             kv_back = lax.psum_scatter(kv_grad, "ctx", scatter_dimension=0, tiled=True).astype(F32)
-        hidden_part, back_mine, back_other, grad_query = query_back(
-            query_grad, query_pre, norm_query, cosine, sine, query_full
-        )
+        next(ffn_steps)
+        if ctx_size == 4:
+            kv_back = scatter4(kv_parts, order.wait(kv_via), core, "ctx", 4, 1, 3, order)
+        kv_back = order.wait(kv_back)
         input_grad, own, send, grad_in, grad_key = input_back(
             kv_back,
             key_pre,
-            norm_key,
+            narrow_gains,
             cosine,
             sine,
-            kv_full,
+            qkv_full,
             hidden_part,
             inputs,
-            norm_in,
+            wide_gains,
             middle_grad,
             hidden,
             back_mine,
@@ -747,8 +916,24 @@
         gain_rows = gain_rows.reshape(4, gain_count, width).astype(BF)
         gain_rows = jnp.pad(gain_rows, ((0, 0), (0, 32 - gain_count), (0, 0)))
         late_parts = late_grads(own, swap_pair(send), gain_rows, model_width)
-        late_sum = ctx_sum(scatter4(late_parts, core, "fsdp", 4, 1, 2), ctx_size, 0)
-        late_other = swap_pair(late_sum)
+        late_steps = reduce_steps(late_parts, core, ctx_size, (), order)
+        chains = {"f": ffn_steps, "l": late_steps}
+        results = {}
+        turns = "lf"
+        while len(results) < 2:
+            for name in turns:
+                if name not in results:
+                    got = next(chains[name])
+                    if got is not None:
+                        results[name] = got
+        (gu_sum, rest_sum), (gu_other, rest_other) = results["f"]
+        (late_sum,), (late_other,) = results["l"]
+        rest_sum, rest_other = rest_sum.T, rest_other.T
+        total_down = join(rest_sum[:unit], rest_other[:unit], core).astype(F32)
+        total_out = join(rest_sum[unit:], rest_other[unit:], core).astype(F32)
+        total_gate = join_cols(gu_sum[:, :unit], gu_other[:, :unit], core)
+        total_up = join_cols(gu_sum[:, unit:], gu_other[:, unit:], core)
+
         query_cols = width - head_size
         total_query = join_cols(
             late_sum[:shard_rows, :query_cols], late_other[:shard_rows, :query_cols], core

time: 242 us -> 217 us (0.90)
  starting transfers between devices: 72 us -> 41.2 us
  local copies, waits for them, and re-layouts: 37.7 us -> 11.7 us
  waiting for transfers between devices: 77.2 us -> 99.7 us
  Pallas kernels: 34.4 us -> 49.6 us
  other arithmetic: 18.3 us -> 12.7 us
    ppermute x50 -> x34, waiting for transfers between devices: 60.9 us -> 86.5 us  [swap(): return lax.ppermute(value, axis, [(i, i ^ flip) for i in range(size)])]
    ppermute x50 -> x34, starting transfers between devices: 58.6 us -> 34.1 us  [swap(): return lax.ppermute(value, axis, [(i, i ^ flip) for i in range(size)])]
    pallas_call x9, Pallas kernels: 34.4 us -> 49.6 us  [kernel_call(): pl.pallas_call(wrapped, out_shape=outs, in_specs=[specs.get(i, pl.BlockSp...]
    unnamed x180 -> x80, local copies, waits for them, and re-layouts: 22.6 us -> 8.09 us
    ppermute x9 -> x5, starting transfers between devices: 13.4 us -> 7.13 us  [swap_split(): return lax.ppermute(value, ('seq', axis), perm)]
    dynamic_slice x5 -> x0, local copies, waits for them, and re-layouts: 4.19 us -> none  [pick_half(): return lax.dynamic_slice_in_dim(value, which * size, size, axis)]
    convert_element_type x4 -> x7, other arithmetic: 0.09 us -> 4.26 us  [the longest x2 3.93 us: reduce_steps(): one = (blocks[1].astype(F32) + jnp.where(core == 0, via, none)).astype(BF)]
    concatenate x1 -> x0, local copies, waits for them, and re-layouts: 4.15 us -> none  [run(): gain_row = jnp.concatenate(gains)]
  transfers between devices with their start and end apart: 59 -> 39, of which waited for: 21 -> 22; matrix products, arithmetic and copies ran while one was open for 11% -> 7% of each run, Pallas kernels for 3% -> 13%
where the time goes in v1:
time: 217 us; the launch traced here: 216 us
  waiting for transfers between devices  99.7 us (46%)
  Pallas kernels  49.6 us (23%)
  starting transfers between devices  41.2 us (19%)
  other arithmetic  12.7 us (6%)
  local copies, waits for them, and re-layouts  11.7 us (5%)
    ppermute x34, waiting for transfers between devices, swap(): return lax.ppermute(value, axis, [(i, i ^ flip) for i in range(size)])  86.5 us
    pallas_call x9, Pallas kernels, kernel_call(): pl.pallas_call(wrapped, out_shape=outs, in_specs=[specs.get(i, pl.BlockSp...  49.6 us
    ppermute x34, starting transfers between devices, swap(): return lax.ppermute(value, axis, [(i, i ^ flip) for i in range(size)])  34.1 us
    ppermute x5, waiting for transfers between devices, swap_split(): return lax.ppermute(value, ('seq', axis), perm)  13.2 us
    unnamed x80, local copies, waits for them, and re-layouts  8.09 us
    ppermute x5, starting transfers between devices, swap_split(): return lax.ppermute(value, ('seq', axis), perm)  7.13 us
  transfers between devices with their start and end apart: 39, of which 22 were waited for; matrix products, arithmetic and copies ran while one was open for 7% of the time, Pallas kernels for 13%

profile of v1, /device:TPU:0, one launch (start us, length us, event | category | flops | bytes accessed | tf_op | source)
XLA Modules:
  0.0 216.3 jit_solution(8692419459657730121)
XLA Ops:
  2.6 3.0 %collective-permute-start = (bf16[96,1536]{1,0:T(8,128)(2,1)}, bf16[96,1536]{1,0:T(8,128)(2,1)S(1)}, u32[]{:S(2)}, u32[]{:S(2)}) collective-permute-start(bf16[96,1536]{1,0:T(8,128)(2,1)} %get-tuple-element.100.refs_1_), channel_id=1, source_target_pairs={{0,1},{1,0},{2,3},{3,2},{4,5},{5,4},{6,7},{7,6},{8,9},{9,8},{10,11... | collective-permute-start | bytes 884744 | tf_op jit(solution)/shard_map/ppermute | solution.py:44
  7.1 3.3 %shard_map.282 = (bf16[640,896]{1,0:T(8,128)(2,1)}, bf16[640,896]{1,0:T(8,128)(2,1)}) custom-call(bf16[640,512]{1,0:T(8,128)(2,1)} %refs_0_.3, bf16[640,512]{1,0:T(8,128)(2,1)} %refs_1_.3, bf16[512,640]{1,0:T(8,128)(2,1)} %refs_2_.3, bf16[256,640]{1,0:T(8,128)(2,1)} %refs_3_.3), custom_call_target="tpu_custom_call" | custom-call | bytes 4587520 | tf_op jit(solution)/shard_map/pallas_call | solution.py:243
  10.5 3.2 %collective-permute-done.refs_2_ = bf16[96,1536]{1,0:T(8,128)(2,1)S(1)} collective-permute-done((bf16[96,1536]{1,0:T(8,128)(2,1)}, bf16[96,1536]{1,0:T(8,128)(2,1)S(1)}, u32[]{:S(2)}, u32[]{:S(2)}) %collective-permute-start) | collective-permute-done | bytes 294944 | tf_op jit(solution)/shard_map/ppermute | solution.py:44
  13.7 7.0 %collective-permute-done.1.refs_3_ = bf16[96,1536]{1,0:T(8,128)(2,1)S(1)} collective-permute-done((bf16[96,1536]{1,0:T(8,128)(2,1)}, bf16[96,1536]{1,0:T(8,128)(2,1)S(1)}, u32[]{:S(2)}, u32[]{:S(2)}) %collective-permute-start.1) | collective-permute-done | bytes 294944 | tf_op jit(solution)/shard_map/ppermute | solution.py:44
  26.7 6.3 %shard_map.281 = (bf16[256,640]{1,0:T(8,128)(2,1)}, f32[256,256]{1,0:T(8,128)}, bf16[272,512]{1,0:T(8,128)(2,1)}, f32[256,1024]{1,0:T(8,128)}, bf16[4,256,256]{2...) custom-call(bf16[256,640]{1,0:T(8,128)(2,1)} %bitcast.15, ...), custom_call_target="tpu_custom_call" | custom-call | flops 503316480 | bytes 7364616 | tf_op jit(solution)/shard_map/pallas_call | solution.py:243
  37.1 5.2 %collective-permute-done.6.refs_2_ = bf16[272,512]{1,0:T(8,128)(2,1)S(1)} collective-permute-done((bf16[272,512]{1,0:T(8,128)(2,1)}, bf16[272,512]{1,0:T(8,128)(2,1)S(1)}, u32[]{:S(2)}, u32[]{:S(2)}) %collective-permute-start.6) | collective-permute-done | bytes 278560 | tf_op jit(solution)/shard_map/ppermute | solution.py:44
  42.3 8.1 %collective-permute-done.7.refs_3_ = bf16[272,512]{1,0:T(8,128)(2,1)S(1)} collective-permute-done((bf16[272,512]{1,0:T(8,128)(2,1)}, bf16[272,512]{1,0:T(8,128)(2,1)S(1)}, u32[]{:S(2)}, u32[]{:S(2)}) %collective-permute-start.7) | collective-permute-done | bytes 278560 | tf_op jit(solution)/shard_map/ppermute | solution.py:44
  53.9 8.4 %collective-permute-done.10.refs_4_ = bf16[272,512]{1,0:T(8,128)(2,1)S(1)} collective-permute-done((bf16[272,512]{1,0:T(8,128)(2,1)S(1)}, bf16[272,512]{1,0:T(8,128)(2,1)S(1)}, u32[]{:S(2)}, u32[]{:S(2)}) %collective-permute-start.10) | collective-permute-done | bytes 278560 | tf_op jit(solution)/shard_map/ppermute | solution.py:54
  62.4 2.8 %shard_map.283 = (bf16[4,256,256]{2,1,0:T(8,128)(2,1)S(1)}, f32[4,256,1]{2,1,0:T(8,128)S(1)}) custom-call(bf16[4,256,256]{2,1,0:T(8,128)(2,1)S(1)} %copy-done.17, bf16[272,512]{1,0:T(8,128)(2,1)S(1)} %copy-done.19, bf16[272,512]{1,0:T(8,128)(2,1)S(1)} %collective-permute-done.6.refs_2_, bf16[272,512]{1,0:T(8,128)(2,1)S(1)} %collective-permute-done.7.refs_3_, ...), custom_call_target="tpu_custom_call" | custom-call | flops 1073741824 | bytes 2166784 | tf_op jit(solution)/shard_map/pallas_call | solution.py:243
  70.4 13.1 %shard_map.284 = (f32[256,640]{1,0:T(8,128)}, f32[256,640]{1,0:T(8,128)S(1)}, bf16[256,5504]{1,0:T(8,128)(2,1)}, bf16[256,5504]{1,0:T(8,128)(2,1)}, bf16[4,256,2...) custom-call(bf16[256,640]{1,0:T(8,128)(2,1)S(1)} %bitcast.16, bf16[256,640]{1,0:T(8,128)(2,1)S(1)} %bitcast.18, ...), custom_call_target="tpu_custom_call" | custom-call | flops 4697620480 | bytes 17887232 | tf_op jit(solution)/shard_map/pallas_call | solution.py:243
  85.3 5.4 %collective-permute-done.15.refs_1_ = bf16[256,5504]{1,0:T(8,128)(2,1)} collective-permute-done((bf16[256,5504]{1,0:T(8,128)(2,1)}, bf16[256,5504]{1,0:T(8,128)(2,1)}, u32[]{:S(2)}, u32[]{:S(2)}) %collective-permute-start.15) | collective-permute-done | bytes 2818080 | tf_op jit(solution)/shard_map/ppermute | solution.py:44
  90.7 6.6 %shard_map.285 = (bf16[640,896]{1,0:T(8,128)(2,1)}, bf16[640,896]{1,0:T(8,128)(2,1)}, bf16[640,896]{1,0:T(8,128)(2,1)}, bf16[640,896]{1,0:T(8,128)(2,1)}) custom-call(bf16[256,5504]{1,0:T(8,128)(2,1)} %get-tuple-element.116.refs_0_, bf16[256,5504]{1,0:T(8,128)(2,1)} %collective-permute-done.15.refs_1_), custom_call_target="tpu_custom_call" | custom-call | flops 2348810240 | bytes 10223616 | tf_op jit(solution)/shard_map/pallas_call | solution.py:243
  98.7 10.2 %shard_map.286 = (bf16[256,512]{1,0:T(8,128)(2,1)}, bf16[256,512]{1,0:T(8,128)(2,1)}, bf16[256,512]{1,0:T(8,128)(2,1)}, bf16[256,512]{1,0:T(8,128)(2,1)}, f32[25...) custom-call(bf16[4,256,256]{2,1,0:T(8,128)(2,1)} %get-tuple-element.102.refs_0_, ...), custom_call_target="tpu_custom_call" | custom-call | flops 2684354560 | bytes 7689216 | tf_op jit(solution)/shard_map/pallas_call | solution.py:243
  110.5 3.1 %collective-permute-done.17 = bf16[640,896]{1,0:T(8,128)(2,1)} collective-permute-done((bf16[640,896]{1,0:T(8,128)(2,1)}, bf16[640,896]{1,0:T(8,128)(2,1)}, u32[]{:S(2)}, u32[]{:S(2)}) %collective-permute-start.17) | collective-permute-done | bytes 1146912 | tf_op jit(solution)/shard_map/ppermute | solution.py:54
  113.7 3.8 %fusion.3 = (bf16[640,896]{1,0:T(8,128)(2,1)}, bf16[640,896]{1,0:T(8,128)(2,1)}) fusion(bf16[640,896]{1,0:T(8,128)(2,1)} %collective-permute-done.17, bf16[640,896]{1,0:T(8,128)(2,1)S(1)} %copy-done.24, pred[]{:T(512)S(6)} %eq.6, bf16[640,896]{1,0:T(8,128)(2,1)} %get-tuple-element.126), kind=kLoop, calls=%fused_computation.5 | loop fusion | flops 5160960 | bytes 5734401 | tf_op jit(solution)/shard_map/convert_element_type | solution.py:105
  123.2 6.7 %collective-permute-done.19 = bf16[256,512]{1,0:T(8,128)(2,1)S(1)} collective-permute-done((bf16[256,512]{1,0:T(8,128)(2,1)S(1)}, bf16[256,512]{1,0:T(8,128)(2,1)S(1)}, u32[]{:S(2)}, u32[]{:S(2)}) %collective-permute-start.19) | collective-permute-done | bytes 262176 | tf_op jit(solution)/shard_map/ppermute | solution.py:44
  132.3 3.4 %shard_map.287 = (f32[256,640]{1,0:T(8,128)}, bf16[256,1408]{1,0:T(8,128)(2,1)S(1)}, bf16[256,1408]{1,0:T(8,128)(2,1)S(1)}, f32[1,640]{1,0:T(1,128)S(1)}, f32[1,256]{1,0:T(1,128)S(1)}) custom-call(f32[256,512]{1,0:T(8,128)S(1)} %convert_add_fusion.2.refs_0_, f32[256,256]{1,0:T(8,128)S(1)} %copy-done.10, f32[16,256]{1,0:T(8,128)S(1)} %copy-done.15, ...), custom_call_target="tpu_custom_call" | custom-call | flops 167772160 | bytes 7663104 | tf_op jit(solution)/shard_map/pallas_call | solution.py:243
  141.1 8.3 %collective-permute-done.22 = bf16[640,896]{1,0:T(8,128)(2,1)} collective-permute-done((bf16[640,896]{1,0:T(8,128)(2,1)}, bf16[640,896]{1,0:T(8,128)(2,1)}, u32[]{:S(2)}, u32[]{:S(2)}) %collective-permute-start.22) | collective-permute-done | bytes 1146912 | tf_op jit(solution)/shard_map/ppermute | solution.py:44
  157.8 7.2 %collective-permute-done.25 = bf16[320,384]{1,0:T(8,128)(2,1)S(1)} collective-permute-done((bf16[320,384]{1,0:T(8,128)(2,1)S(1)}, bf16[320,384]{1,0:T(8,128)(2,1)S(1)}, u32[]{:S(2)}, u32[]{:S(2)}) %collective-permute-start.25) | collective-permute-done | bytes 245792 | tf_op jit(solution)/shard_map/ppermute | solution.py:44
  169.0 8.3 %collective-permute-done.29 = bf16[160,384]{1,0:T(8,128)(2,1)S(1)} collective-permute-done((bf16[160,384]{1,0:T(8,128)(2,1)S(1)}, bf16[160,384]{1,0:T(8,128)(2,1)S(1)}, u32[]{:S(2)}, u32[]{:S(2)}) %collective-permute-start.29) | collective-permute-done | bytes 122912 | tf_op jit(solution)/shard_map/ppermute | solution.py:44
  179.7 3.1 %collective-permute-done.28 = bf16[192,768]{1,0:T(8,128)(2,1)S(1)} collective-permute-done((bf16[192,768]{1,0:T(8,128)(2,1)S(1)}, bf16[192,768]{1,0:T(8,128)(2,1)S(1)}, u32[]{:S(2)}, u32[]{:S(2)}) %collective-permute-start.28) | collective-permute-done | bytes 294944 | tf_op jit(solution)/shard_map/ppermute | solution.py:44
  185.2 10.1 %collective-permute-done.32 = bf16[160,384]{1,0:T(8,128)(2,1)S(1)} collective-permute-done((bf16[160,384]{1,0:T(8,128)(2,1)S(1)}, bf16[160,384]{1,0:T(8,128)(2,1)S(1)}, u32[]{:S(2)}, u32[]{:S(2)}) %collective-permute-start.32) | collective-permute-done | bytes 122912 | tf_op jit(solution)/shard_map/ppermute | solution.py:44
  196.0 2.7 %collective-permute-start.35 = (bf16[320,384]{1,0:T(8,128)(2,1)S(1)}, bf16[320,384]{1,0:T(8,128)(2,1)S(1)}, u32[]{:S(2)}, u32[]{:S(2)}) collective-permute-start(bf16[320,384]{1,0:T(8,128)(2,1)S(1)} %maximum_select_fusion.8), channel_id=1, source_target_pairs={{0,12},{4,8},{8,4},{12,0},{1,13},{5,9},{9,5},{13,1},{2,14},{6,10},... | collective-permute-start | bytes 737288 | tf_op jit(solution)/shard_map/ppermute | solution.py:44
  198.9 7.4 %collective-permute-done.35 = bf16[320,384]{1,0:T(8,128)(2,1)S(1)} collective-permute-done((bf16[320,384]{1,0:T(8,128)(2,1)S(1)}, bf16[320,384]{1,0:T(8,128)(2,1)S(1)}, u32[]{:S(2)}, u32[]{:S(2)}) %collective-permute-start.35) | collective-permute-done | bytes 245792 | tf_op jit(solution)/shard_map/ppermute | solution.py:44
  (199 shorter events, 68.3 us)
Async XLA Ops:
  2.6 11.1 %collective-permute-start = (bf16[96,1536]{1,0:T(8,128)(2,1)}, bf16[96,1536]{1,0:T(8,128)(2,1)S(1)}, u32[]{:S(2)}, u32[]{:S(2)}) collective-permute-start(bf16[96,1536]{1,0:T(8,128)(2,1)} %get-tuple-element.100.refs_1_), channel_id=1, source_target_pairs={{0,1},{1,0},{2,3},{3,2},{4,5},{5,4},{6,7},{7,6},{8,9},{9,8},{10,11... | collective-permute-start | bytes 884744 | tf_op jit(solution)/shard_map/ppermute | solution.py:44
  5.6 15.0 %collective-permute-start.1 = (bf16[96,1536]{1,0:T(8,128)(2,1)}, bf16[96,1536]{1,0:T(8,128)(2,1)S(1)}, u32[]{:S(2)}, u32[]{:S(2)}) collective-permute-start(bf16[96,1536]{1,0:T(8,128)(2,1)} %get-tuple-element.100.refs_1_), channel_id=1, source_target_pairs={{0,2},{1,3},{2,0},{3,1},{4,6},{5,7},{6,4},{7,5},{8,10},{9,11},{10,... | collective-permute-start | bytes 884744 | tf_op jit(solution)/shard_map/ppermute | solution.py:44
  7.1 13.5 %collective-permute-start.2 = (bf16[96,1536]{1,0:T(8,128)(2,1)}, bf16[96,1536]{1,0:T(8,128)(2,1)}, u32[]{:S(2)}, u32[]{:S(2)}) collective-permute-start(bf16[96,1536]{1,0:T(8,128)(2,1)} %get-tuple-element.100.refs_1_), channel_id=1, source_target_pairs={{0,3},{1,2},{2,1},{3,0},{4,7},{5,6},{6,5},{7,4},{8,11},{9,10},{10,... | collective-permute-start | bytes 884744 | tf_op jit(solution)/shard_map/ppermute | solution.py:44
  20.6 29.8 %collective-permute-start.8 = (bf16[640,896]{1,0:T(8,128)(2,1)}, bf16[640,896]{1,0:T(8,128)(2,1)S(1)}, u32[]{:S(2)}, u32[]{:S(2)}) collective-permute-start(bf16[640,896]{1,0:T(8,128)(2,1)} %get-tuple-element.105.refs_3_), channel_id=1, source_target_pairs={{0,1},{1,0},{2,3},{3,2},{4,5},{5,4},{6,7},{7,6},{8,9},{9,8},{10,11... | collective-permute-start | bytes 3440648 | tf_op jit(solution)/shard_map/ppermute | solution.py:44
  21.9 28.5 %collective-permute-start.9 = (bf16[640,896]{1,0:T(8,128)(2,1)}, bf16[640,896]{1,0:T(8,128)(2,1)}, u32[]{:S(2)}, u32[]{:S(2)}) collective-permute-start(bf16[640,896]{1,0:T(8,128)(2,1)} %get-tuple-element.105.refs_3_), channel_id=1, source_target_pairs={{0,2},{1,3},{2,0},{3,1},{4,6},{5,7},{6,4},{7,5},{8,10},{9,11},{10,... | collective-permute-start | bytes 3440648 | tf_op jit(solution)/shard_map/ppermute | solution.py:44
  34.6 15.7 %collective-permute-start.7 = (bf16[272,512]{1,0:T(8,128)(2,1)}, bf16[272,512]{1,0:T(8,128)(2,1)S(1)}, u32[]{:S(2)}, u32[]{:S(2)}) collective-permute-start(bf16[272,512]{1,0:T(8,128)(2,1)} %get-tuple-element.103.refs_1_), channel_id=1, source_target_pairs={{0,12},{4,8},{8,4},{12,0},{1,13},{5,9},{9,5},{13,1},{2,14},{6,10},... | collective-permute-start | bytes 835592 | tf_op jit(solution)/shard_map/ppermute | solution.py:44
  50.6 15.9 %collective-permute-start.11 = (bf16[640,896]{1,0:T(8,128)(2,1)S(1)}, bf16[640,896]{1,0:T(8,128)(2,1)S(1)}, u32[]{:S(2)}, u32[]{:S(2)}) collective-permute-start(bf16[640,896]{1,0:T(8,128)(2,1)S(1)} %broadcast_select_fusion), channel_id=1, source_target_pairs={{0,2},{1,3},{2,0},{3,1},{16,17},{17,16},{18,19},{19,18},{4,6},{5,7... | collective-permute-start | bytes 3440648 | tf_op jit(solution)/shard_map/ppermute | solution.py:54
  53.4 13.2 %collective-permute-start.12 = (bf16[640,896]{1,0:T(8,128)(2,1)S(1)}, bf16[640,896]{1,0:T(8,128)(2,1)S(1)}, u32[]{:S(2)}, u32[]{:S(2)}) collective-permute-start(bf16[640,896]{1,0:T(8,128)(2,1)S(1)} %collective-permute-done.8.refs_4_), channel_id=1, source_target_pairs={{0,16},{16,0},{1,17},{17,1},{2,18},{18,2},{3,19},{19,3},{4,20},{20... | collective-permute-start | bytes 3440648 | tf_op jit(solution)/shard_map/ppermute | solution.py:44
  53.4 13.2 %collective-permute-start.13 = (bf16[640,896]{1,0:T(8,128)(2,1)}, bf16[640,896]{1,0:T(8,128)(2,1)S(1)}, u32[]{:S(2)}, u32[]{:S(2)}) collective-permute-start(bf16[640,896]{1,0:T(8,128)(2,1)} %collective-permute-done.9.refs_5_), channel_id=1, source_target_pairs={{0,16},{16,0},{1,17},{17,1},{2,18},{18,2},{3,19},{19,3},{4,20},{20... | collective-permute-start | bytes 3440648 | tf_op jit(solution)/shard_map/ppermute | solution.py:44
  97.4 16.2 %collective-permute-start.17 = (bf16[640,896]{1,0:T(8,128)(2,1)}, bf16[640,896]{1,0:T(8,128)(2,1)}, u32[]{:S(2)}, u32[]{:S(2)}) collective-permute-start(bf16[640,896]{1,0:T(8,128)(2,1)} %get-tuple-element.127), channel_id=1, source_target_pairs={{0,2},{1,3},{2,0},{3,1},{16,17},{17,16},{18,19},{19,18},{4,6},{5,7... | collective-permute-start | bytes 3440648 | tf_op jit(solution)/shard_map/ppermute | solution.py:54
  118.9 11.0 %collective-permute-start.19 = (bf16[256,512]{1,0:T(8,128)(2,1)S(1)}, bf16[256,512]{1,0:T(8,128)(2,1)S(1)}, u32[]{:S(2)}, u32[]{:S(2)}) collective-permute-start(bf16[256,512]{1,0:T(8,128)(2,1)S(1)} %get-tuple-element.135), channel_id=1, source_target_pairs={{0,12},{4,8},{8,4},{12,0},{1,13},{5,9},{9,5},{13,1},{2,14},{6,10},... | collective-permute-start | bytes 786440 | tf_op jit(solution)/shard_map/ppermute | solution.py:44
  120.3 11.8 %collective-permute-start.18 = (bf16[256,512]{1,0:T(8,128)(2,1)S(1)}, bf16[256,512]{1,0:T(8,128)(2,1)S(1)}, u32[]{:S(2)}, u32[]{:S(2)}) collective-permute-start(bf16[256,512]{1,0:T(8,128)(2,1)S(1)} %get-tuple-element.133), channel_id=1, source_target_pairs={{0,4},{4,0},{8,12},{12,8},{1,5},{5,1},{9,13},{13,9},{2,6},{6,2},{1... | collective-permute-start | bytes 786440 | tf_op jit(solution)/shard_map/ppermute | solution.py:44
  121.0 28.4 %collective-permute-start.22 = (bf16[640,896]{1,0:T(8,128)(2,1)}, bf16[640,896]{1,0:T(8,128)(2,1)}, u32[]{:S(2)}, u32[]{:S(2)}) collective-permute-start(bf16[640,896]{1,0:T(8,128)(2,1)} %get-tuple-element.130), channel_id=1, source_target_pairs={{0,1},{1,0},{2,3},{3,2},{4,5},{5,4},{6,7},{7,6},{8,9},{9,8},{10,11... | collective-permute-start | bytes 3440648 | tf_op jit(solution)/shard_map/ppermute | solution.py:44
  121.7 27.7 %collective-permute-start.23 = (bf16[640,896]{1,0:T(8,128)(2,1)}, bf16[640,896]{1,0:T(8,128)(2,1)}, u32[]{:S(2)}, u32[]{:S(2)}) collective-permute-start(bf16[640,896]{1,0:T(8,128)(2,1)} %get-tuple-element.131), channel_id=1, source_target_pairs={{0,2},{1,3},{2,0},{3,1},{4,6},{5,7},{6,4},{7,5},{8,10},{9,11},{10,... | collective-permute-start | bytes 3440648 | tf_op jit(solution)/shard_map/ppermute | solution.py:44
  139.8 15.8 %collective-permute-start.21 = (bf16[192,768]{1,0:T(8,128)(2,1)S(1)}, bf16[192,768]{1,0:T(8,128)(2,1)S(1)}, u32[]{:S(2)}, u32[]{:S(2)}) collective-permute-start(bf16[192,768]{1,0:T(8,128)(2,1)S(1)} %get-tuple-element.153), channel_id=1, source_target_pairs={{0,2},{1,3},{2,0},{3,1},{16,17},{17,16},{18,19},{19,18},{4,6},{5,7... | collective-permute-start | bytes 884744 | tf_op jit(solution)/shard_map/ppermute | solution.py:54
  151.9 13.2 %collective-permute-start.26 = (bf16[320,512]{1,0:T(8,128)(2,1)S(1)}, bf16[320,512]{1,0:T(8,128)(2,1)S(1)}, u32[]{:S(2)}, u32[]{:S(2)}) collective-permute-start(bf16[320,512]{1,0:T(8,128)(2,1)S(1)} %dynamic-slice_convert_fusion), channel_id=1, source_target_pairs={{0,4},{4,0},{8,12},{12,8},{1,5},{5,1},{9,13},{13,9},{2,6},{6,2},{1... | collective-permute-start | bytes 983048 | tf_op jit(solution)/shard_map/ppermute | solution.py:44
  153.1 11.9 %collective-permute-start.25 = (bf16[320,384]{1,0:T(8,128)(2,1)S(1)}, bf16[320,384]{1,0:T(8,128)(2,1)S(1)}, u32[]{:S(2)}, u32[]{:S(2)}) collective-permute-start(bf16[320,384]{1,0:T(8,128)(2,1)S(1)} %dynamic-slice_convert_fusion.1), channel_id=1, source_target_pairs={{0,12},{4,8},{8,4},{12,0},{1,13},{5,9},{9,5},{13,1},{2,14},{6,10},... | collective-permute-start | bytes 737288 | tf_op jit(solution)/shard_map/ppermute | solution.py:44
  155.7 12.2 %collective-permute-start.24 = (bf16[192,768]{1,0:T(8,128)(2,1)S(1)}, bf16[192,768]{1,0:T(8,128)(2,1)S(1)}, u32[]{:S(2)}, u32[]{:S(2)}) collective-permute-start(bf16[192,768]{1,0:T(8,128)(2,1)S(1)} %get-tuple-element.159), channel_id=1, source_target_pairs={{0,1},{1,0},{2,3},{3,2},{4,5},{5,4},{6,7},{7,6},{8,9},{9,8},{10,11... | collective-permute-start | bytes 884744 | tf_op jit(solution)/shard_map/ppermute | solution.py:44
  156.7 11.3 %collective-permute-start.27 = (bf16[192,768]{1,0:T(8,128)(2,1)S(1)}, bf16[192,768]{1,0:T(8,128)(2,1)S(1)}, u32[]{:S(2)}, u32[]{:S(2)}) collective-permute-start(bf16[192,768]{1,0:T(8,128)(2,1)S(1)} %get-tuple-element.161), channel_id=1, source_target_pairs={{0,2},{1,3},{2,0},{3,1},{4,6},{5,7},{6,4},{7,5},{8,10},{9,11},{10,... | collective-permute-start | bytes 884744 | tf_op jit(solution)/shard_map/ppermute | solution.py:44
  165.2 12.0 %collective-permute-start.30 = (bf16[160,512]{1,0:T(8,128)(2,1)S(1)}, bf16[160,512]{1,0:T(8,128)(2,1)S(1)}, u32[]{:S(2)}, u32[]{:S(2)}) collective-permute-start(bf16[160,512]{1,0:T(8,128)(2,1)S(1)} %dynamic-slice_convert_fusion.2), channel_id=1, source_target_pairs={{0,12},{4,8},{8,4},{12,0},{1,13},{5,9},{9,5},{13,1},{2,14},{6,10},... | collective-permute-start | bytes 491528 | tf_op jit(solution)/shard_map/ppermute | solution.py:44
  168.1 14.7 %collective-permute-start.28 = (bf16[192,768]{1,0:T(8,128)(2,1)S(1)}, bf16[192,768]{1,0:T(8,128)(2,1)S(1)}, u32[]{:S(2)}, u32[]{:S(2)}) collective-permute-start(bf16[192,768]{1,0:T(8,128)(2,1)S(1)} %add_convert_fusion.2), channel_id=1, source_target_pairs={{0,4},{4,0},{8,12},{12,8},{1,5},{5,1},{9,13},{13,9},{2,6},{6,2},{1... | collective-permute-start | bytes 884744 | tf_op jit(solution)/shard_map/ppermute | solution.py:44
  182.9 15.9 %collective-permute-start.31 = (bf16[192,768]{1,0:T(8,128)(2,1)S(1)}, bf16[192,768]{1,0:T(8,128)(2,1)S(1)}, u32[]{:S(2)}, u32[]{:S(2)}) collective-permute-start(bf16[192,768]{1,0:T(8,128)(2,1)S(1)} %add_convert_fusion.1), channel_id=1, source_target_pairs={{0,12},{4,8},{8,4},{12,0},{1,13},{5,9},{9,5},{13,1},{2,14},{6,10},... | collective-permute-start | bytes 884744 | tf_op jit(solution)/shard_map/ppermute | solution.py:44
  184.9 10.5 %collective-permute-start.32 = (bf16[160,384]{1,0:T(8,128)(2,1)S(1)}, bf16[160,384]{1,0:T(8,128)(2,1)S(1)}, u32[]{:S(2)}, u32[]{:S(2)}) collective-permute-start(bf16[160,384]{1,0:T(8,128)(2,1)S(1)} %add_convert_fusion.4), channel_id=1, source_target_pairs={{0,4},{4,0},{8,12},{12,8},{1,5},{5,1},{9,13},{13,9},{2,6},{6,2},{1... | collective-permute-start | bytes 368648 | tf_op jit(solution)/shard_map/ppermute | solution.py:44
  195.3 11.2 %collective-permute-start.36 = (bf16[320,512]{1,0:T(8,128)(2,1)S(1)}, bf16[320,512]{1,0:T(8,128)(2,1)S(1)}, u32[]{:S(2)}, u32[]{:S(2)}) collective-permute-start(bf16[320,512]{1,0:T(8,128)(2,1)S(1)} %maximum_select_fusion.5), channel_id=1, source_target_pairs={{0,4},{4,0},{8,12},{12,8},{1,5},{5,1},{9,13},{13,9},{2,6},{6,2},{1... | collective-permute-start | bytes 983048 | tf_op jit(solution)/shard_map/ppermute | solution.py:44
  (54 other events, 474.0 us)

commit v2 on v1

--- a/solution.py
+++ b/solution.py
@@ -54,14 +54,19 @@
     return lax.ppermute(value, ("seq", axis), perm)
 
 
-def scatter4(blocks, via, core, axis, size, first, second, order):
-    via = via.astype(F32)
-    none = jnp.zeros_like(via)
-    one = (blocks[1].astype(F32) + jnp.where(core == 0, via, none)).astype(BF)
-    two = (blocks[2].astype(F32) + jnp.where(core == 0, none, via)).astype(BF)
-    one = swap(order(one), axis, first, size).astype(F32)
-    two = swap(order(two), axis, second, size).astype(F32)
-    return blocks[0].astype(F32) + one + two
+def by_core(core, one, two):
+    return jnp.where(core == 0, one, two), jnp.where(core == 0, two, one)
+
+
+def scatter4(blocks, axis, size, first, second, order, at_once=False):
+    own, passing, both = blocks
+    both = swap_split(both if at_once else order(both), axis, size, second, first)
+    yield
+    both = order.wait(both)
+    passing = (passing.astype(F32) + both[1].astype(F32)).astype(BF)
+    passing = swap_split(order(passing), axis, size, first, second)
+    yield
+    yield own.astype(F32) + order.wait(passing).astype(F32) + both[0].astype(F32)
 
 
 def halves(value, pick):
@@ -92,23 +97,15 @@
         return lax.optimization_barrier((value, self.last))[0]
 
 
-def reduce_steps(blocks, core, ctx_size, cuts, order):
+def reduce_steps(blocks, ctx_size, cuts, order):
     place = lax.axis_index("ctx")
     high = place // 2
     odd = lax.rem(place, 2)
     mixed = lax.rem(high + odd, 2)
     steps = [(1, mixed), (3, high)]
-    via = swap_split(order(blocks[3]), "fsdp", 4, 2, 1)
-    yield
-    via = order.wait(via).astype(F32)
-    none = jnp.zeros_like(via)
-    one = (blocks[1].astype(F32) + jnp.where(core == 0, via, none)).astype(BF)
-    two = (blocks[2].astype(F32) + jnp.where(core == 0, none, via)).astype(BF)
-    one = swap(order(one), "fsdp", 1, 4)
-    two = swap(order(two), "fsdp", 2, 4)
-    yield
-    one, two = order.wait(one), order.wait(two)
-    value = blocks[0].astype(F32) + one.astype(F32) + two.astype(F32)
+    for value in scatter4(blocks, "fsdp", 4, 1, 2, order):
+        if value is None:
+            yield
     if ctx_size != 4:
         value = lax.psum(value.astype(BF), "ctx")
     elif not cuts:
@@ -449,7 +446,7 @@
     def body(*refs):
         q, blocks, refs = refs[0], refs[1 : 1 + count], refs[1 + count :]
         lse, grads, pre, g_query, cos, sin, full = refs[:7]
-        kv_grads, (hidden_part, mine, other, gain_grad, kv_acc) = refs[7 : 7 + count], refs[7 + count :]
+        kv_grads, (hidden_part, mine, other, gain_grad, kv_acc) = refs[7:10], refs[10:]
         core = lax.axis_index("seq")
         query_grads, gains, hidden = [], None, None
         masks = tile_masks(blocks, rows)
@@ -488,13 +485,17 @@
             gains = gain if gains is None else gains + gain
             part = inner_cols(back, full[:, at])
             hidden = part if hidden is None else hidden + part
-        for i in range(count):
-            kv_grads[i][...] = kv_acc[i].astype(BF)
+        one, two = by_core(core, kv_acc[1], kv_acc[2])
+        kv_grads[0][...] = kv_acc[0].astype(BF)
+        kv_grads[1][...] = one.astype(BF)
+        kv_grads[2][0] = two.astype(BF)
+        kv_grads[2][1] = kv_acc[3].astype(BF)
         hidden_part[...] = hidden
         split_heads(query_grads, core, mine, other, size)
         gain_grad[...] = gains
 
-    outs = [shape((rows, 2 * size), BF)] * count + [
+    block = (rows, 2 * size)
+    outs = [shape(block, BF), shape(block, BF), shape((2, *block), BF)] + [
         shape((rows, width), F32),
         shape((rows, per * size), BF),
         shape((rows, per * size), BF),
@@ -509,7 +510,7 @@
         10 * heads * rows * rows * count * size,
         scratch=[pltpu.VMEM((count, rows, 2 * size), F32)],
         far=tuple(range(2 + count)) + tuple(k + count for k in (3, 5, 6, 7)),
-        back=tuple(range(3 + count)),
+        back=tuple(range(6)),
         room=62,
     )
 
@@ -649,15 +650,20 @@
 
         at = lambda k, j, size: slice(offs[k] + j * size, offs[k] + (j + 1) * size)
         whole = lambda k: slice(offs[k], offs[k] + width)
-        for j, out in enumerate(outs):
-            out[:, :unit] = product(whole(0), at(4, j, unit))
-            out[:, unit : 2 * unit] = product(whole(0), at(5, j, unit))
-            out[:, 2 * unit : 3 * unit] = product(whole(1), at(3, j, unit))
-            out[:, 3 * unit :] = product(whole(2), at(6, j, half))
-
-    outs = [shape((width, 3 * unit + half), BF)] * 4
+        core = lax.axis_index("seq")
+        for left, k, size, start in ((0, 4, unit, 0), (0, 5, unit, 1), (1, 3, unit, 2), (2, 6, half, 3)):
+            cols = slice(start * unit, start * unit + size)
+            own, one, two, far = [product(whole(left), at(k, j, size)) for j in range(4)]
+            one, two = by_core(core, one, two)
+            outs[0][:, cols] = own
+            outs[1][:, cols] = one
+            outs[2][0, :, cols] = two
+            outs[2][1, :, cols] = far
+
+    block = (width, 3 * unit + half)
+    outs = [shape(block, BF), shape(block, BF), shape((2, *block), BF)]
     flops = 4 * rows * width * 4 * (3 * unit + half)
-    return kernel_call(body, outs, [own, got], flops, far=(0, 1), back=tuple(range(4)), room=62)
+    return kernel_call(body, outs, [own, got], flops, far=(0, 1), back=(0, 1, 2), room=62)
 
 
 def query_back(query_grad, query_pre, norm_query, cosine, sine, query_full):
@@ -744,19 +750,44 @@
     shard = width // 4
 
     def body(a, b, extra, *refs):
-        outs, total = refs[:4], refs[4]
+        outs, total = refs[:3], refs[3]
         place = lax.axis_index("fsdp")
         total[...] = inner_rows(a[:, :width], a[:, width:]) + inner_rows(b[:, :width], b[:, width:])
-        for flip, out in enumerate(outs):
+        core = lax.axis_index("seq")
+        for order, out in enumerate((outs[0], outs[1], outs[2].at[0], outs[2].at[1])):
+            flip = order if order in (0, 3) else jnp.where(core == 0, order, 3 - order)
             out[:shard, :] = total[rows_at((place ^ flip) * shard, shard, 16), :].astype(BF)
             out[shard:, :] = extra[place ^ flip]
 
-    outs = [shape((shard + gains.shape[1], out_cols), BF)] * 4
+    block = (shard + gains.shape[1], out_cols)
+    outs = [shape(block, BF), shape(block, BF), shape((2, *block), BF)]
     flops = 4 * rows * width * out_cols
     scratch = [pltpu.VMEM((width, out_cols), F32)]
     return kernel_call(
-        body, outs, [own, got, gains], flops, scratch, far=(0, 1), back=tuple(range(4))
+        body, outs, [own, got, gains], flops, scratch, far=(0, 1), back=(0, 1, 2)
     )
+
+
+def finish(gu_sum, gu_other, rest_sum, rest_other, unit, half):
+    width = gu_sum.shape[0]
+
+    def body(gu_a, gu_b, rest_a, rest_b, gate, up, down, out):
+        core = lax.axis_index("seq")
+        low, high = by_core(core, gu_a[...], gu_b[...])
+        gate[:, :unit] = low[:, :unit].astype(F32)
+        gate[:, unit:] = high[:, :unit].astype(F32)
+        up[:, :unit] = low[:, unit:].astype(F32)
+        up[:, unit:] = high[:, unit:].astype(F32)
+        low, high = by_core(core, rest_a[...], rest_b[...])
+        down[:unit, :] = low[:, :unit].T.astype(F32)
+        down[unit:, :] = high[:, :unit].T.astype(F32)
+        out[:half, :] = low[:, unit:].T.astype(F32)
+        out[half:, :] = high[:, unit:].T.astype(F32)
+
+    outs = [shape((width, 2 * unit), F32)] * 2
+    outs += [shape((2 * unit, width), F32), shape((2 * half, width), F32)]
+    args = [gu_sum, gu_other, rest_sum, rest_other]
+    return kernel_call(body, outs, args, 0, back=(0, 1, 2, 3), room=24)
 
 
 def pick_half(value, which, axis):
@@ -854,7 +885,7 @@
 
         parts = ffn_weight_grads(own, swap_pair(send), offs, unit, head_size // 2)
         order = Order()
-        ffn_steps = reduce_steps(parts, core, ctx_size, (2 * unit,), order)
+        ffn_steps = reduce_steps(parts, ctx_size, (2 * unit,), order)
         next(ffn_steps)
         context_grad = after(context_grad, parts[0])
 
@@ -871,7 +902,8 @@
                 sine,
                 qkv_full,
             )
-            kv_via = swap_split(kv_parts[3], "ctx", 4, 3, 1)
+            kv_steps = scatter4(kv_parts, "ctx", 4, 1, 3, order, True)
+            next(kv_steps)
         else:
             query_grad, key_grad, value_grad = attend_backward(
                 by_row,
@@ -889,9 +921,11 @@
                 query_grad, query_pre, narrow_gains, cosine, sine, qkv_full
             )
             kv_back = lax.psum_scatter(kv_grad, "ctx", scatter_dimension=0, tiled=True).astype(F32)
+        if ctx_size == 4:
+            next(kv_steps)
         next(ffn_steps)
         if ctx_size == 4:
-            kv_back = scatter4(kv_parts, order.wait(kv_via), core, "ctx", 4, 1, 3, order)
+            kv_back = next(kv_steps)
         kv_back = order.wait(kv_back)
         input_grad, own, send, grad_in, grad_key = input_back(
             kv_back,
@@ -916,30 +950,24 @@
         gain_rows = gain_rows.reshape(4, gain_count, width).astype(BF)
         gain_rows = jnp.pad(gain_rows, ((0, 0), (0, 32 - gain_count), (0, 0)))
         late_parts = late_grads(own, swap_pair(send), gain_rows, model_width)
-        late_steps = reduce_steps(late_parts, core, ctx_size, (), order)
-        chains = {"f": ffn_steps, "l": late_steps}
-        results = {}
-        turns = "lf"
-        while len(results) < 2:
-            for name in turns:
-                if name not in results:
-                    got = next(chains[name])
-                    if got is not None:
-                        results[name] = got
-        (gu_sum, rest_sum), (gu_other, rest_other) = results["f"]
-        (late_sum,), (late_other,) = results["l"]
-        rest_sum, rest_other = rest_sum.T, rest_other.T
-        total_down = join(rest_sum[:unit], rest_other[:unit], core).astype(F32)
-        total_out = join(rest_sum[unit:], rest_other[unit:], core).astype(F32)
-        total_gate = join_cols(gu_sum[:, :unit], gu_other[:, :unit], core)
-        total_up = join_cols(gu_sum[:, unit:], gu_other[:, unit:], core)
-
+        late_steps = reduce_steps(late_parts, ctx_size, (), order)
+        for _ in range(4 if ctx_size == 4 else 2):
+            next(late_steps)
+            if ctx_size == 4:
+                next(ffn_steps)
+        next(late_steps)
+        (late_sum,), (late_other,) = next(late_steps)
         query_cols = width - head_size
         total_query = join_cols(
             late_sum[:shard_rows, :query_cols], late_other[:shard_rows, :query_cols], core
         )
         total_key = jnp.where(core == 0, late_sum, late_other)[:shard_rows, query_cols:].astype(F32)
         total_value = jnp.where(core == 0, late_other, late_sum)[:shard_rows, query_cols:].astype(F32)
+        next(ffn_steps)
+        (gu_sum, rest_sum), (gu_other, rest_other) = next(ffn_steps)
+        total_gate, total_up, total_down, total_out = finish(
+            gu_sum, gu_other, rest_sum, rest_other, unit, head_size // 2
+        )
         gain_at = slice(shard_rows, shard_rows + gain_count)
         gain_total = (late_sum[gain_at].astype(F32) + late_other[gain_at].astype(F32)).reshape(-1)
         outs = []

time: 217 us -> 213 us (0.982)
  Pallas kernels: 49.6 us -> 53.5 us
  waiting for transfers between devices: 99.7 us -> 96.5 us
    ppermute x34 -> x28, waiting for transfers between devices: 86.5 us -> 68.6 us  [swap(): return lax.ppermute(value, axis, [(i, i ^ flip) for i in range(size)])]
    ppermute x5 -> x8, waiting for transfers between devices: 13.2 us -> 27.9 us  [swap_split(): return lax.ppermute(value, ('seq', axis), perm)]
    pallas_call x9 -> x10, Pallas kernels: 49.6 us -> 53.5 us  [kernel_call(): pl.pallas_call(wrapped, out_shape=outs, in_specs=[specs.get(i, pl.BlockSp...]
    ppermute x34 -> x28, starting transfers between devices: 34.1 us -> 30.7 us  [swap(): return lax.ppermute(value, axis, [(i, i ^ flip) for i in range(size)])]
    ppermute x5 -> x8, starting transfers between devices: 7.13 us -> 9.19 us  [swap_split(): return lax.ppermute(value, ('seq', axis), perm)]
    unnamed x80 -> x76, local copies, waits for them, and re-layouts: 8.09 us -> 8.29 us
    convert_element_type x5 -> x3, other arithmetic: 4.36 us -> 4.16 us  [scatter4(): passing = (passing.astype(F32) + both[1].astype(F32)).astype(BF)]
  transfers between devices with their start and end apart: 39 -> 36, of which waited for: 22 -> 21; matrix products, arithmetic and copies ran while one was open for 7% -> 6% of each run, Pallas kernels for 13% -> 13%
where the time goes in v2:
time: 213 us
  waiting for transfers between devices  96.5 us (45%)
  Pallas kernels  53.5 us (25%)
  starting transfers between devices  39.9 us (19%)
  other arithmetic  10.8 us (5%)
  local copies, waits for them, and re-layouts  10.6 us (5%)
    ppermute x28, waiting for transfers between devices, swap(): return lax.ppermute(value, axis, [(i, i ^ flip) for i in range(size)])  68.6 us
    pallas_call x10, Pallas kernels, kernel_call(): pl.pallas_call(wrapped, out_shape=outs, in_specs=[specs.get(i, pl.BlockSp...  53.5 us
    ppermute x28, starting transfers between devices, swap(): return lax.ppermute(value, axis, [(i, i ^ flip) for i in range(size)])  30.7 us
    ppermute x8, waiting for transfers between devices, swap_split(): return lax.ppermute(value, ('seq', axis), perm)  27.9 us
    ppermute x8, starting transfers between devices, swap_split(): return lax.ppermute(value, ('seq', axis), perm)  9.19 us
    unnamed x76, local copies, waits for them, and re-layouts  8.29 us
  transfers between devices with their start and end apart: 36, of which 21 were waited for; matrix products, arithmetic and copies ran while one was open for 6% of the time, Pallas kernels for 13%

profile of v2, /device:TPU:0, one launch (start us, length us, event | category | flops | bytes accessed | tf_op | source)
XLA Modules:
  0.0 212.8 jit_solution(1682089378559485683)
XLA Ops:
  2.6 3.0 %collective-permute-start = (bf16[96,1536]{1,0:T(8,128)(2,1)}, bf16[96,1536]{1,0:T(8,128)(2,1)S(1)}, u32[]{:S(2)}, u32[]{:S(2)}) collective-permute-start(bf16[96,1536]{1,0:T(8,128)(2,1)} %get-tuple-element.97.refs_1_), channel_id=1, source_target_pairs={{0,1},{1,0},{2,3},{3,2},{4,5},{5,4},{6,7},{7,6},{8,9},{9,8},{10,11... | collective-permute-start | bytes 884744 | tf_op jit(solution)/shard_map/ppermute | solution.py:44
  7.1 3.3 %shard_map.282 = (bf16[640,896]{1,0:T(8,128)(2,1)}, bf16[640,896]{1,0:T(8,128)(2,1)}) custom-call(bf16[640,512]{1,0:T(8,128)(2,1)} %refs_0_.3, bf16[640,512]{1,0:T(8,128)(2,1)} %refs_1_.3, bf16[512,640]{1,0:T(8,128)(2,1)} %refs_2_.3, bf16[256,640]{1,0:T(8,128)(2,1)} %refs_3_.3), custom_call_target="tpu_custom_call" | custom-call | bytes 4587520 | tf_op jit(solution)/shard_map/pallas_call | solution.py:240
  10.5 3.2 %collective-permute-done.refs_2_ = bf16[96,1536]{1,0:T(8,128)(2,1)S(1)} collective-permute-done((bf16[96,1536]{1,0:T(8,128)(2,1)}, bf16[96,1536]{1,0:T(8,128)(2,1)S(1)}, u32[]{:S(2)}, u32[]{:S(2)}) %collective-permute-start) | collective-permute-done | bytes 294944 | tf_op jit(solution)/shard_map/ppermute | solution.py:44
  13.7 7.0 %collective-permute-done.1.refs_3_ = bf16[96,1536]{1,0:T(8,128)(2,1)S(1)} collective-permute-done((bf16[96,1536]{1,0:T(8,128)(2,1)}, bf16[96,1536]{1,0:T(8,128)(2,1)S(1)}, u32[]{:S(2)}, u32[]{:S(2)}) %collective-permute-start.1) | collective-permute-done | bytes 294944 | tf_op jit(solution)/shard_map/ppermute | solution.py:44
  27.5 6.3 %shard_map.281 = (bf16[256,640]{1,0:T(8,128)(2,1)}, f32[256,256]{1,0:T(8,128)}, bf16[272,512]{1,0:T(8,128)(2,1)}, f32[256,1024]{1,0:T(8,128)}, bf16[4,256,256]{2...) custom-call(bf16[256,640]{1,0:T(8,128)(2,1)} %bitcast.31, ...), custom_call_target="tpu_custom_call" | custom-call | flops 503316480 | bytes 7364616 | tf_op jit(solution)/shard_map/pallas_call | solution.py:240
  37.9 5.2 %collective-permute-done.6.refs_2_ = bf16[272,512]{1,0:T(8,128)(2,1)S(1)} collective-permute-done((bf16[272,512]{1,0:T(8,128)(2,1)}, bf16[272,512]{1,0:T(8,128)(2,1)S(1)}, u32[]{:S(2)}, u32[]{:S(2)}) %collective-permute-start.6) | collective-permute-done | bytes 278560 | tf_op jit(solution)/shard_map/ppermute | solution.py:44
  43.0 8.1 %collective-permute-done.7.refs_3_ = bf16[272,512]{1,0:T(8,128)(2,1)S(1)} collective-permute-done((bf16[272,512]{1,0:T(8,128)(2,1)}, bf16[272,512]{1,0:T(8,128)(2,1)S(1)}, u32[]{:S(2)}, u32[]{:S(2)}) %collective-permute-start.7) | collective-permute-done | bytes 278560 | tf_op jit(solution)/shard_map/ppermute | solution.py:44
  54.6 8.5 %collective-permute-done.10.refs_4_ = bf16[272,512]{1,0:T(8,128)(2,1)S(1)} collective-permute-done((bf16[272,512]{1,0:T(8,128)(2,1)S(1)}, bf16[272,512]{1,0:T(8,128)(2,1)S(1)}, u32[]{:S(2)}, u32[]{:S(2)}) %collective-permute-start.10) | collective-permute-done | bytes 278560 | tf_op jit(solution)/shard_map/ppermute | solution.py:54
  63.1 2.8 %shard_map.283 = (bf16[4,256,256]{2,1,0:T(8,128)(2,1)S(1)}, f32[4,256,1]{2,1,0:T(8,128)S(1)}) custom-call(bf16[4,256,256]{2,1,0:T(8,128)(2,1)S(1)} %copy-done.19, bf16[272,512]{1,0:T(8,128)(2,1)S(1)} %copy-done.21, bf16[272,512]{1,0:T(8,128)(2,1)S(1)} %collective-permute-done.6.refs_2_, bf16[272,512]{1,0:T(8,128)(2,1)S(1)} %collective-permute-done.7.refs_3_, ...), custom_call_target="tpu_custom_call" | custom-call | flops 1073741824 | bytes 2166784 | tf_op jit(solution)/shard_map/pallas_call | solution.py:240
  71.2 13.2 %shard_map.284 = (f32[256,640]{1,0:T(8,128)}, f32[256,640]{1,0:T(8,128)S(1)}, bf16[256,5504]{1,0:T(8,128)(2,1)}, bf16[256,5504]{1,0:T(8,128)(2,1)}, bf16[4,256,2...) custom-call(bf16[256,640]{1,0:T(8,128)(2,1)S(1)} %bitcast.32, bf16[256,640]{1,0:T(8,128)(2,1)S(1)} %bitcast.34, ...), custom_call_target="tpu_custom_call" | custom-call | flops 4697620480 | bytes 17887232 | tf_op jit(solution)/shard_map/pallas_call | solution.py:240
  86.1 5.4 %collective-permute-done.15.refs_1_ = bf16[256,5504]{1,0:T(8,128)(2,1)} collective-permute-done((bf16[256,5504]{1,0:T(8,128)(2,1)}, bf16[256,5504]{1,0:T(8,128)(2,1)}, u32[]{:S(2)}, u32[]{:S(2)}) %collective-permute-start.15) | collective-permute-done | bytes 2818080 | tf_op jit(solution)/shard_map/ppermute | solution.py:44
  91.5 7.4 %shard_map.285 = (bf16[640,896]{1,0:T(8,128)(2,1)}, bf16[640,896]{1,0:T(8,128)(2,1)}, bf16[2,640,896]{2,1,0:T(8,128)(2,1)}) custom-call(bf16[256,5504]{1,0:T(8,128)(2,1)} %get-tuple-element.113.refs_0_, bf16[256,5504]{1,0:T(8,128)(2,1)} %collective-permute-done.15.refs_1_), custom_call_target="tpu_custom_call" | custom-call | flops 2348810240 | bytes 10223616 | tf_op jit(solution)/shard_map/pallas_call | solution.py:240
  100.1 10.2 %shard_map.286 = (bf16[256,512]{1,0:T(8,128)(2,1)}, bf16[256,512]{1,0:T(8,128)(2,1)}, bf16[2,256,512]{2,1,0:T(8,128)(2,1)}, f32[256,640]{1,0:T(8,128)}, bf16[256...) custom-call(bf16[4,256,256]{2,1,0:T(8,128)(2,1)} %get-tuple-element.99.refs_0_, ...), custom_call_target="tpu_custom_call" | custom-call | flops 2684354560 | bytes 7689216 | tf_op jit(solution)/shard_map/pallas_call | solution.py:240
  111.9 13.9 %collective-permute-done.16 = bf16[2,256,512]{2,1,0:T(8,128)(2,1)S(1)} collective-permute-done((bf16[2,256,512]{2,1,0:T(8,128)(2,1)}, bf16[2,256,512]{2,1,0:T(8,128)(2,1)S(1)}, u32[]{:S(2)}, u32[]{:S(2)}) %collective-permute-start.16) | collective-permute-done | bytes 524320 | tf_op jit(solution)/shard_map/ppermute | solution.py:54
  127.5 3.0 %fusion = bf16[640,896]{1,0:T(8,128)(2,1)} fusion(bf16[640,896]{1,0:T(8,128)(2,1)} %get-tuple-element.126, bf16[2,640,896]{2,1,0:T(8,128)(2,1)} %collective-permute-done.18), kind=kLoop, calls=%fused_computation.2 | loop fusion | flops 2293760 | bytes 3440640 | tf_op jit(solution)/shard_map/convert_element_type | solution.py:66
  133.7 3.7 %shard_map.287 = (f32[256,640]{1,0:T(8,128)}, bf16[256,1408]{1,0:T(8,128)(2,1)S(1)}, bf16[256,1408]{1,0:T(8,128)(2,1)}, f32[1,640]{1,0:T(1,128)S(1)}, f32[1,256]{1,0:T(1,128)S(1)}) custom-call(f32[256,512]{1,0:T(8,128)S(1)} %convert_add_fusion.5.refs_0_, f32[256,256]{1,0:T(8,128)S(1)} %copy-done.10, f32[16,256]{1,0:T(8,128)S(1)} %copy-done.15, ...), custom_call_target="tpu_custom_call" | custom-call | flops 167772160 | bytes 7663104 | tf_op jit(solution)/shard_map/pallas_call | solution.py:240
  149.4 3.0 %collective-permute-start.24 = (bf16[320,512]{1,0:T(8,128)(2,1)S(1)}, bf16[320,512]{1,0:T(8,128)(2,1)S(1)}, u32[]{:S(2)}, u32[]{:S(2)}) collective-permute-start(bf16[320,512]{1,0:T(8,128)(2,1)S(1)} %dynamic-slice_convert_fusion), channel_id=1, source_target_pairs={{0,4},{4,0},{8,12},{12,8},{1,5},{5,1},{9,13},{13,9},{2,6},{6,2},{1... | collective-permute-start | bytes 983048 | tf_op jit(solution)/shard_map/ppermute | solution.py:44
  155.6 8.5 %collective-permute-done.23 = bf16[320,384]{1,0:T(8,128)(2,1)S(1)} collective-permute-done((bf16[320,384]{1,0:T(8,128)(2,1)S(1)}, bf16[320,384]{1,0:T(8,128)(2,1)S(1)}, u32[]{:S(2)}, u32[]{:S(2)}) %collective-permute-start.23) | collective-permute-done | bytes 245792 | tf_op jit(solution)/shard_map/ppermute | solution.py:44
  167.8 5.6 %collective-permute-done.26 = bf16[160,384]{1,0:T(8,128)(2,1)S(1)} collective-permute-done((bf16[160,384]{1,0:T(8,128)(2,1)S(1)}, bf16[160,384]{1,0:T(8,128)(2,1)S(1)}, u32[]{:S(2)}, u32[]{:S(2)}) %collective-permute-start.26) | collective-permute-done | bytes 122912 | tf_op jit(solution)/shard_map/ppermute | solution.py:44
  173.4 3.5 %collective-permute-start.30 = (bf16[160,512]{1,0:T(8,128)(2,1)S(1)}, bf16[160,512]{1,0:T(8,128)(2,1)S(1)}, u32[]{:S(2)}, u32[]{:S(2)}) collective-permute-start(bf16[160,512]{1,0:T(8,128)(2,1)S(1)} %add_convert_fusion.2), channel_id=1, source_target_pairs={{0,12},{4,8},{8,4},{12,0},{1,13},{5,9},{9,5},{13,1},{2,14},{6,10},... | collective-permute-start | bytes 491528 | tf_op jit(solution)/shard_map/ppermute | solution.py:44
  176.9 3.3 %collective-permute-done.25 = bf16[192,768]{1,0:T(8,128)(2,1)S(1)} collective-permute-done((bf16[192,768]{1,0:T(8,128)(2,1)S(1)}, bf16[192,768]{1,0:T(8,128)(2,1)S(1)}, u32[]{:S(2)}, u32[]{:S(2)}) %collective-permute-start.25) | collective-permute-done | bytes 294944 | tf_op jit(solution)/shard_map/ppermute | solution.py:44
  180.2 4.9 %collective-permute-start.28 = (bf16[192,768]{1,0:T(8,128)(2,1)S(1)}, bf16[192,768]{1,0:T(8,128)(2,1)S(1)}, u32[]{:S(2)}, u32[]{:S(2)}) collective-permute-start(bf16[192,768]{1,0:T(8,128)(2,1)S(1)} %add_convert_fusion.1), channel_id=1, source_target_pairs={{0,12},{4,8},{8,4},{12,0},{1,13},{5,9},{9,5},{13,1},{2,14},{6,10},... | collective-permute-start | bytes 884744 | tf_op jit(solution)/shard_map/ppermute | solution.py:44
  185.2 10.0 %collective-permute-done.29 = bf16[160,384]{1,0:T(8,128)(2,1)S(1)} collective-permute-done((bf16[160,384]{1,0:T(8,128)(2,1)S(1)}, bf16[160,384]{1,0:T(8,128)(2,1)S(1)}, u32[]{:S(2)}, u32[]{:S(2)}) %collective-permute-start.29) | collective-permute-done | bytes 122912 | tf_op jit(solution)/shard_map/ppermute | solution.py:44
  198.1 7.9 %collective-permute-done.34 = bf16[320,384]{1,0:T(8,128)(2,1)S(1)} collective-permute-done((bf16[320,384]{1,0:T(8,128)(2,1)S(1)}, bf16[320,384]{1,0:T(8,128)(2,1)S(1)}, u32[]{:S(2)}, u32[]{:S(2)}) %collective-permute-start.34) | collective-permute-done | bytes 245792 | tf_op jit(solution)/shard_map/ppermute | solution.py:44
  (181 shorter events, 60.6 us)
Async XLA Ops:
  2.6 11.1 %collective-permute-start = (bf16[96,1536]{1,0:T(8,128)(2,1)}, bf16[96,1536]{1,0:T(8,128)(2,1)S(1)}, u32[]{:S(2)}, u32[]{:S(2)}) collective-permute-start(bf16[96,1536]{1,0:T(8,128)(2,1)} %get-tuple-element.97.refs_1_), channel_id=1, source_target_pairs={{0,1},{1,0},{2,3},{3,2},{4,5},{5,4},{6,7},{7,6},{8,9},{9,8},{10,11... | collective-permute-start | bytes 884744 | tf_op jit(solution)/shard_map/ppermute | solution.py:44
  5.6 15.0 %collective-permute-start.1 = (bf16[96,1536]{1,0:T(8,128)(2,1)}, bf16[96,1536]{1,0:T(8,128)(2,1)S(1)}, u32[]{:S(2)}, u32[]{:S(2)}) collective-permute-start(bf16[96,1536]{1,0:T(8,128)(2,1)} %get-tuple-element.97.refs_1_), channel_id=1, source_target_pairs={{0,2},{1,3},{2,0},{3,1},{4,6},{5,7},{6,4},{7,5},{8,10},{9,11},{10,... | collective-permute-start | bytes 884744 | tf_op jit(solution)/shard_map/ppermute | solution.py:44
  7.1 13.5 %collective-permute-start.2 = (bf16[96,1536]{1,0:T(8,128)(2,1)}, bf16[96,1536]{1,0:T(8,128)(2,1)S(1)}, u32[]{:S(2)}, u32[]{:S(2)}) collective-permute-start(bf16[96,1536]{1,0:T(8,128)(2,1)} %get-tuple-element.97.refs_1_), channel_id=1, source_target_pairs={{0,3},{1,2},{2,1},{3,0},{4,7},{5,6},{6,5},{7,4},{8,11},{9,10},{10,... | collective-permute-start | bytes 884744 | tf_op jit(solution)/shard_map/ppermute | solution.py:44
  21.4 29.8 %collective-permute-start.8 = (bf16[640,896]{1,0:T(8,128)(2,1)}, bf16[640,896]{1,0:T(8,128)(2,1)S(1)}, u32[]{:S(2)}, u32[]{:S(2)}) collective-permute-start(bf16[640,896]{1,0:T(8,128)(2,1)} %get-tuple-element.102.refs_3_), channel_id=1, source_target_pairs={{0,1},{1,0},{2,3},{3,2},{4,5},{5,4},{6,7},{7,6},{8,9},{9,8},{10,11... | collective-permute-start | bytes 3440648 | tf_op jit(solution)/shard_map/ppermute | solution.py:44
  22.6 28.7 %collective-permute-start.9 = (bf16[640,896]{1,0:T(8,128)(2,1)}, bf16[640,896]{1,0:T(8,128)(2,1)}, u32[]{:S(2)}, u32[]{:S(2)}) collective-permute-start(bf16[640,896]{1,0:T(8,128)(2,1)} %get-tuple-element.102.refs_3_), channel_id=1, source_target_pairs={{0,2},{1,3},{2,0},{3,1},{4,6},{5,7},{6,4},{7,5},{8,10},{9,11},{10,... | collective-permute-start | bytes 3440648 | tf_op jit(solution)/shard_map/ppermute | solution.py:44
  33.8 9.3 %collective-permute-start.6 = (bf16[272,512]{1,0:T(8,128)(2,1)}, bf16[272,512]{1,0:T(8,128)(2,1)S(1)}, u32[]{:S(2)}, u32[]{:S(2)}) collective-permute-start(bf16[272,512]{1,0:T(8,128)(2,1)} %get-tuple-element.100.refs_1_), channel_id=1, source_target_pairs={{0,4},{4,0},{8,12},{12,8},{1,5},{5,1},{9,13},{13,9},{2,6},{6,2},{1... | collective-permute-start | bytes 835592 | tf_op jit(solution)/shard_map/ppermute | solution.py:44
  35.4 15.7 %collective-permute-start.7 = (bf16[272,512]{1,0:T(8,128)(2,1)}, bf16[272,512]{1,0:T(8,128)(2,1)S(1)}, u32[]{:S(2)}, u32[]{:S(2)}) collective-permute-start(bf16[272,512]{1,0:T(8,128)(2,1)} %get-tuple-element.100.refs_1_), channel_id=1, source_target_pairs={{0,12},{4,8},{8,4},{12,0},{1,13},{5,9},{9,5},{13,1},{2,14},{6,10},... | collective-permute-start | bytes 835592 | tf_op jit(solution)/shard_map/ppermute | solution.py:44
  51.4 15.9 %collective-permute-start.11 = (bf16[640,896]{1,0:T(8,128)(2,1)S(1)}, bf16[640,896]{1,0:T(8,128)(2,1)S(1)}, u32[]{:S(2)}, u32[]{:S(2)}) collective-permute-start(bf16[640,896]{1,0:T(8,128)(2,1)S(1)} %broadcast_select_fusion), channel_id=1, source_target_pairs={{0,2},{1,3},{2,0},{3,1},{16,17},{17,16},{18,19},{19,18},{4,6},{5,7... | collective-permute-start | bytes 3440648 | tf_op jit(solution)/shard_map/ppermute | solution.py:54
  52.6 10.5 %collective-permute-start.10 = (bf16[272,512]{1,0:T(8,128)(2,1)S(1)}, bf16[272,512]{1,0:T(8,128)(2,1)S(1)}, u32[]{:S(2)}, u32[]{:S(2)}) collective-permute-start(bf16[272,512]{1,0:T(8,128)(2,1)S(1)} %broadcast_select_fusion.1), channel_id=1, source_target_pairs={{0,12},{4,8},{8,4},{12,0},{16,20},{20,16},{24,28},{28,24},{1,13},{... | collective-permute-start | bytes 835592 | tf_op jit(solution)/shard_map/ppermute | solution.py:54
  54.1 13.3 %collective-permute-start.12 = (bf16[640,896]{1,0:T(8,128)(2,1)S(1)}, bf16[640,896]{1,0:T(8,128)(2,1)S(1)}, u32[]{:S(2)}, u32[]{:S(2)}) collective-permute-start(bf16[640,896]{1,0:T(8,128)(2,1)S(1)} %collective-permute-done.8.refs_4_), channel_id=1, source_target_pairs={{0,16},{16,0},{1,17},{17,1},{2,18},{18,2},{3,19},{19,3},{4,20},{20... | collective-permute-start | bytes 3440648 | tf_op jit(solution)/shard_map/ppermute | solution.py:44
  54.1 13.3 %collective-permute-start.13 = (bf16[640,896]{1,0:T(8,128)(2,1)}, bf16[640,896]{1,0:T(8,128)(2,1)S(1)}, u32[]{:S(2)}, u32[]{:S(2)}) collective-permute-start(bf16[640,896]{1,0:T(8,128)(2,1)} %collective-permute-done.9.refs_5_), channel_id=1, source_target_pairs={{0,16},{16,0},{1,17},{17,1},{2,18},{18,2},{3,19},{19,3},{4,20},{20... | collective-permute-start | bytes 3440648 | tf_op jit(solution)/shard_map/ppermute | solution.py:44
  98.9 28.5 %collective-permute-start.18 = (bf16[2,640,896]{2,1,0:T(8,128)(2,1)}, bf16[2,640,896]{2,1,0:T(8,128)(2,1)}, u32[]{:S(2)}, u32[]{:S(2)}) collective-permute-start(bf16[2,640,896]{2,1,0:T(8,128)(2,1)} %get-tuple-element.123), channel_id=1, source_target_pairs={{0,2},{1,3},{2,0},{3,1},{16,17},{17,16},{18,19},{19,18},{4,6},{5,7... | collective-permute-start | bytes 6881288 | tf_op jit(solution)/shard_map/ppermute | solution.py:54
  110.3 15.5 %collective-permute-start.16 = (bf16[2,256,512]{2,1,0:T(8,128)(2,1)}, bf16[2,256,512]{2,1,0:T(8,128)(2,1)S(1)}, u32[]{:S(2)}, u32[]{:S(2)}) collective-permute-start(bf16[2,256,512]{2,1,0:T(8,128)(2,1)} %get-tuple-element.122), channel_id=1, source_target_pairs={{0,12},{4,8},{8,4},{12,0},{16,20},{20,16},{24,28},{28,24},{1,13},{... | collective-permute-start | bytes 1572872 | tf_op jit(solution)/shard_map/ppermute | solution.py:54
  130.5 16.3 %collective-permute-start.21 = (bf16[640,896]{1,0:T(8,128)(2,1)}, bf16[640,896]{1,0:T(8,128)(2,1)}, u32[]{:S(2)}, u32[]{:S(2)}) collective-permute-start(bf16[640,896]{1,0:T(8,128)(2,1)} %fusion), channel_id=1, source_target_pairs={{0,1},{1,0},{2,3},{3,2},{16,18},{17,19},{18,16},{19,17},{4,5},{5,4... | collective-permute-start | bytes 3440648 | tf_op jit(solution)/shard_map/ppermute | solution.py:54
  143.8 9.9 %collective-permute-start.20 = (bf16[2,192,768]{2,1,0:T(8,128)(2,1)S(1)}, bf16[2,192,768]{2,1,0:T(8,128)(2,1)S(1)}, u32[]{:S(2)}, u32[]{:S(2)}) collective-permute-start(bf16[2,192,768]{2,1,0:T(8,128)(2,1)S(1)} %get-tuple-element.147), channel_id=1, source_target_pairs={{0,2},{1,3},{2,0},{3,1},{16,17},{17,16},{18,19},{19,18},{4,6},{5,7... | collective-permute-start | bytes 1769480 | tf_op jit(solution)/shard_map/ppermute | solution.py:54
  149.4 14.8 %collective-permute-start.24 = (bf16[320,512]{1,0:T(8,128)(2,1)S(1)}, bf16[320,512]{1,0:T(8,128)(2,1)S(1)}, u32[]{:S(2)}, u32[]{:S(2)}) collective-permute-start(bf16[320,512]{1,0:T(8,128)(2,1)S(1)} %dynamic-slice_convert_fusion), channel_id=1, source_target_pairs={{0,4},{4,0},{8,12},{12,8},{1,5},{5,1},{9,13},{13,9},{2,6},{6,2},{1... | collective-permute-start | bytes 983048 | tf_op jit(solution)/shard_map/ppermute | solution.py:44
  152.4 11.7 %collective-permute-start.23 = (bf16[320,384]{1,0:T(8,128)(2,1)S(1)}, bf16[320,384]{1,0:T(8,128)(2,1)S(1)}, u32[]{:S(2)}, u32[]{:S(2)}) collective-permute-start(bf16[320,384]{1,0:T(8,128)(2,1)S(1)} %dynamic-slice_convert_fusion.1), channel_id=1, source_target_pairs={{0,12},{4,8},{8,4},{12,0},{1,13},{5,9},{9,5},{13,1},{2,14},{6,10},... | collective-permute-start | bytes 737288 | tf_op jit(solution)/shard_map/ppermute | solution.py:44
  153.9 13.6 %collective-permute-start.22 = (bf16[192,768]{1,0:T(8,128)(2,1)S(1)}, bf16[192,768]{1,0:T(8,128)(2,1)S(1)}, u32[]{:S(2)}, u32[]{:S(2)}) collective-permute-start(bf16[192,768]{1,0:T(8,128)(2,1)S(1)} %fusion.2), channel_id=1, source_target_pairs={{0,1},{1,0},{2,3},{3,2},{16,18},{17,19},{18,16},{19,17},{4,5},{5,4... | collective-permute-start | bytes 884744 | tf_op jit(solution)/shard_map/ppermute | solution.py:54
  164.3 9.1 %collective-permute-start.27 = (bf16[160,512]{1,0:T(8,128)(2,1)S(1)}, bf16[160,512]{1,0:T(8,128)(2,1)S(1)}, u32[]{:S(2)}, u32[]{:S(2)}) collective-permute-start(bf16[160,512]{1,0:T(8,128)(2,1)S(1)} %dynamic-slice_convert_fusion.2), channel_id=1, source_target_pairs={{0,12},{4,8},{8,4},{12,0},{1,13},{5,9},{9,5},{13,1},{2,14},{6,10},... | collective-permute-start | bytes 491528 | tf_op jit(solution)/shard_map/ppermute | solution.py:44
  167.6 12.5 %collective-permute-start.25 = (bf16[192,768]{1,0:T(8,128)(2,1)S(1)}, bf16[192,768]{1,0:T(8,128)(2,1)S(1)}, u32[]{:S(2)}, u32[]{:S(2)}) collective-permute-start(bf16[192,768]{1,0:T(8,128)(2,1)S(1)} %fusion.1), channel_id=1, source_target_pairs={{0,4},{4,0},{8,12},{12,8},{1,5},{5,1},{9,13},{13,9},{2,6},{6,2},{1... | collective-permute-start | bytes 884744 | tf_op jit(solution)/shard_map/ppermute | solution.py:44
  173.4 11.7 %collective-permute-start.30 = (bf16[160,512]{1,0:T(8,128)(2,1)S(1)}, bf16[160,512]{1,0:T(8,128)(2,1)S(1)}, u32[]{:S(2)}, u32[]{:S(2)}) collective-permute-start(bf16[160,512]{1,0:T(8,128)(2,1)S(1)} %add_convert_fusion.2), channel_id=1, source_target_pairs={{0,12},{4,8},{8,4},{12,0},{1,13},{5,9},{9,5},{13,1},{2,14},{6,10},... | collective-permute-start | bytes 491528 | tf_op jit(solution)/shard_map/ppermute | solution.py:44
  180.2 17.7 %collective-permute-start.28 = (bf16[192,768]{1,0:T(8,128)(2,1)S(1)}, bf16[192,768]{1,0:T(8,128)(2,1)S(1)}, u32[]{:S(2)}, u32[]{:S(2)}) collective-permute-start(bf16[192,768]{1,0:T(8,128)(2,1)S(1)} %add_convert_fusion.1), channel_id=1, source_target_pairs={{0,12},{4,8},{8,4},{12,0},{1,13},{5,9},{9,5},{13,1},{2,14},{6,10},... | collective-permute-start | bytes 884744 | tf_op jit(solution)/shard_map/ppermute | solution.py:44
  185.1 10.1 %collective-permute-start.29 = (bf16[160,384]{1,0:T(8,128)(2,1)S(1)}, bf16[160,384]{1,0:T(8,128)(2,1)S(1)}, u32[]{:S(2)}, u32[]{:S(2)}) collective-permute-start(bf16[160,384]{1,0:T(8,128)(2,1)S(1)} %add_convert_fusion.3), channel_id=1, source_target_pairs={{0,4},{4,0},{8,12},{12,8},{1,5},{5,1},{9,13},{13,9},{2,6},{6,2},{1... | collective-permute-start | bytes 368648 | tf_op jit(solution)/shard_map/ppermute | solution.py:44
  195.3 10.9 %collective-permute-start.32 = (bf16[320,512]{1,0:T(8,128)(2,1)S(1)}, bf16[320,512]{1,0:T(8,128)(2,1)S(1)}, u32[]{:S(2)}, u32[]{:S(2)}) collective-permute-start(bf16[320,512]{1,0:T(8,128)(2,1)S(1)} %maximum_select_fusion.2), channel_id=1, source_target_pairs={{0,4},{4,0},{8,12},{12,8},{1,5},{5,1},{9,13},{13,9},{2,6},{6,2},{1... | collective-permute-start | bytes 983048 | tf_op jit(solution)/shard_map/ppermute | solution.py:44
  (50 other events, 268.3 us)
